TPU v7x, 128 devices: a whole 4x4x4 slice. The times are simulated.
128 devices in a mesh: kv: 4 (over y), seq: 32 (over z, x, core).
Axes of the slice: x: 4, y: 4, z: 4, core: 2. Of those that a mesh axis runs over, the one named last changes fastest.
Arguments:
- page_cache: bfloat16 [2048, 2, 8, 128, 128], P('seq', None, 'kv'), may hold values from -9 to 64
- keep_list: int32 [2048, 128], P('seq'), may hold values from 0 to 1, as said below
- fold_weight: float32 [2048, 128], P('seq'), may hold values from 0.1 to 10
- page_table: int32 [256, 8], replicated, may hold values from 0 to 2047, as said below
- lengths: int32 [256], replicated, may hold values from 1 to 1024, 163840 in all
- queries: bfloat16 [256, 16, 128], P('seq', 'kv'), may hold values from -6 to 40
- fresh_entries: bfloat16 [256, 2, 8, 128], P('seq', None, 'kv'), may hold values from -6 to 6
- out_weight: bfloat16 [2048, 2048], P('kv'), may hold values from -0.125 to 0.125
Outputs:
- packed_cache: bfloat16 [2048, 2, 8, 128, 128], P('seq', None, 'kv')
- packed_mass: bfloat16 [2048, 128], P('seq')
- attended: bfloat16 [256, 2048], P('seq', 'kv')
- projected: bfloat16 [256, 2048], P('seq', 'kv')
Inputs may be any that keep to these rules, and one draw needn't show every extreme that they name: `page_table`: every physical page appears exactly once. Of the 64 pages of the requests held by one index of seq, exactly 2 lie on each index of seq. `keep_list`: every page keeps at least one and drops at least one of its 128 slots.
All inputs are finite; a program needn't handle non-finite values.
Results may differ from a plain program's by a relative error of at most 0.015.
Values may be sent and summed in bfloat16 or wider, within the bound.
A program may use at most 128 MiB of HBM per device.

v0:
```python
import jax
import jax.numpy as jnp
from jax import lax
from jax.sharding import PartitionSpec as P

negative_floor = -1e30


def compact_pages(page_cache, keep_list, fold_weight, valid_count):
    slot_count = keep_list.shape[1]
    slot_index = jnp.arange(slot_count, dtype=jnp.int32)
    valid = slot_index[None, :] < valid_count[:, None]
    kept_mask = jnp.logical_and(valid, keep_list > 0)
    dropped = jnp.logical_and(valid, keep_list == 0)
    kept_flag = kept_mask.astype(jnp.int32)
    position = jnp.cumsum(kept_flag, axis=1) - kept_flag
    total_kept = jnp.sum(kept_flag, axis=1)
    selector = jnp.logical_and(
        position[:, None, :] == slot_index[None, :, None], kept_mask[:, None, :]
    ).astype(jnp.bfloat16)
    moved = jnp.einsum(
        "pst,pchtd->pchsd", selector, page_cache, preferred_element_type=jnp.float32
    ).astype(jnp.bfloat16)
    dropped_weight = jnp.where(dropped, fold_weight, 0.0)
    weight_sum = jnp.sum(dropped_weight, axis=1)
    folded = jnp.einsum(
        "pt,pchtd->pchd",
        dropped_weight,
        page_cache.astype(jnp.float32),
        precision=lax.Precision.HIGHEST,
    )
    folded = (folded / jnp.maximum(weight_sum, 1.0)[:, None, None, None]).astype(jnp.bfloat16)
    at_fold = slot_index[None, :] == total_kept[:, None]
    packed = jnp.where(at_fold[:, None, None, :, None], folded[:, :, :, None, :], moved)
    page_mass = jnp.where(
        slot_index[None, :] < total_kept[:, None], 1.0, jnp.where(at_fold, weight_sum[:, None], 0.0)
    ).astype(jnp.bfloat16)
    return (packed, page_mass)


def page_partials(query_pages, pages, page_mass, score_scale):
    scores = (
        jnp.einsum("phgd,phtd->phgt", query_pages, pages[:, 0], preferred_element_type=jnp.float32)
        * score_scale
    )
    live_mask = (page_mass > 0)[:, None, None, :]
    page_top = jnp.max(jnp.where(live_mask, scores, negative_floor), axis=-1)
    weights = jnp.where(
        live_mask,
        page_mass.astype(jnp.float32)[:, None, None, :] * jnp.exp(scores - page_top[..., None]),
        0.0,
    )
    page_total = jnp.sum(weights, axis=-1)
    page_part = jnp.einsum(
        "phgt,phtd->phgd",
        weights.astype(jnp.bfloat16),
        pages[:, 1],
        preferred_element_type=jnp.float32,
    )
    return (page_top, page_total, page_part)


def per_device(
    page_cache, keep_list, fold_weight, page_table, lengths, queries, fresh_entries, out_weight
):
    seq_count = lax.axis_size("seq")
    seq_rank = lax.axis_index("seq")
    pages_dev = page_cache.shape[0]
    peer_pages = pages_dev // seq_count
    req_dev = queries.shape[0]
    max_pages = page_table.shape[1]
    slot_count = keep_list.shape[1]
    kv_local = page_cache.shape[2]
    head_size = queries.shape[2]
    groups = queries.shape[1] // kv_local
    score_scale = head_size ** (-0.5)
    table_flat = page_table.reshape(-1)
    all_pages = table_flat.shape[0]
    holder = (table_flat // pages_dev).reshape(seq_count, pages_dev)
    earlier = jnp.arange(pages_dev)[None, :] < jnp.arange(pages_dev)[:, None]
    within = jnp.sum(
        jnp.logical_and(holder[:, :, None] == holder[:, None, :], earlier[None]), axis=2
    )
    slot_rows = (holder * peer_pages + within).reshape(-1)
    within_flat = within.reshape(-1)
    logical = (
        jnp.zeros((all_pages,), jnp.int32)
        .at[table_flat]
        .set(jnp.arange(all_pages, dtype=jnp.int32))
    )
    mine_logical = lax.dynamic_slice_in_dim(logical, seq_rank * pages_dev, pages_dev)
    owner = mine_logical // pages_dev
    send_row = owner * peer_pages + within_flat[mine_logical]
    send_order = jnp.argsort(send_row)
    request = mine_logical // max_pages
    valid_count = jnp.clip(lengths[request] - mine_logical % max_pages * slot_count, 0, slot_count)
    packed, page_mass = compact_pages(page_cache, keep_list, fold_weight, valid_count)
    own_rows = lax.dynamic_slice_in_dim(slot_rows, seq_rank * pages_dev, pages_dev)
    query_groups = queries.reshape(req_dev, kv_local, groups, head_size)
    query_pages = jnp.broadcast_to(
        query_groups[:, None], (req_dev, max_pages, kv_local, groups, head_size)
    ).reshape(pages_dev, kv_local, groups, head_size)
    moved, moved_mass = (
        lax.all_to_all(packed[send_order], "seq", split_axis=0, concat_axis=0, tiled=True),
        lax.all_to_all(page_mass[send_order], "seq", split_axis=0, concat_axis=0, tiled=True),
    )
    page_top, page_total, page_part = page_partials(
        query_pages, moved[own_rows], moved_mass[own_rows], score_scale
    )
    page_top = page_top.reshape(req_dev, max_pages, kv_local, groups)
    page_total = page_total.reshape(req_dev, max_pages, kv_local, groups)
    page_part = page_part.reshape(req_dev, max_pages, kv_local, groups, head_size)
    own_score = (
        jnp.einsum(
            "rhgd,rhd->rhg", query_groups, fresh_entries[:, 0], preferred_element_type=jnp.float32
        )
        * score_scale
    )
    best_score = jnp.maximum(jnp.max(page_top, axis=1), own_score)
    factor = jnp.exp(page_top - best_score[:, None])
    own_factor = jnp.exp(own_score - best_score)
    denominator = jnp.sum(factor * page_total, axis=1) + own_factor
    fresh_value = fresh_entries[:, 1].astype(jnp.float32)
    numerator = (
        jnp.sum(factor[..., None] * page_part, axis=1)
        + own_factor[..., None] * fresh_value[:, :, None, :]
    )
    attended = (
        (numerator / denominator[..., None])
        .astype(jnp.bfloat16)
        .reshape(req_dev, kv_local * groups * head_size)
    )
    partial_value = jnp.dot(attended, out_weight, preferred_element_type=jnp.float32)
    projected = lax.psum_scatter(
        partial_value.astype(jnp.bfloat16), "kv", scatter_dimension=1, tiled=True
    )
    return (packed, page_mass, attended, projected)


def solution(mesh):
    placed = (
        P("seq", None, "kv", None, None),
        P("seq", None),
        P("seq", None),
        P(),
        P(),
        P("seq", "kv", None),
        P("seq", None, "kv", None),
        P("kv", None),
    )
    return jax.shard_map(
        per_device,
        mesh=mesh,
        in_specs=placed,
        out_specs=(
            P("seq", None, "kv", None, None),
            P("seq", None),
            P("seq", "kv"),
            P("seq", "kv"),
        ),
        check_vma=False,
    )
```

profile of v0, /device:TPU:1, one launch (start us, length us, event | category | flops | bytes accessed | tf_op | source)
XLA Modules:
  0.0 210.4 jit_solution(13599703098330460998)
XLA Ops:
  7.2 1.0 copy.22
  8.2 0.1 reshape.196
  8.3 0.1 reshape.195
  8.4 0.9 convert_reduce_fusion
  9.5 8.0 %scatter_custom_fusion = s32[2048]{0:T(1024)S(1)} fusion(s32[2048]{0:T(1024)S(1)} %bitcast.68, s32[2048]{0:T(1024)S(1)} %iota.33, s32[]{:T(128)} %constant.67.clone.1), kind=kCustom, calls=%fused_computation.65 | custom fusion | bytes 8196 | tf_op jit(solution)/shard_map/scatter | solution.py:89
  17.6 0.8 gather_fusion.1
  18.4 1.5 gather_fusion
  19.9 0.8 fusion.27
  20.7 0.3 reduce_window_sum.11
  21.0 1.0 fusion.29
  22.0 2.0 sort.17
  24.0 0.1 convert_subtract_fusion
  24.2 0.1 select_convert_fusion
  24.3 1.2 gather_fusion.2
  25.5 9.4 %all-to-all-start = ((bf16[32,2,128]{2,1,0:T(2,128)(2,1)}), bf16[32,2,128]{2,1,0:T(2,128)(2,1)S(1)}, u32[]{:S(2)}, u32[]{:S(2)}) async-start(bf16[32,2,128]{2,1,0:T(2,128)(2,1)} %bitcast.8), calls=%async_computation | async-start | bytes 32768 | tf_op jit(solution)/shard_map/all_to_all | solution.py:105
  35.0 5.7 %fusion.31 = f32[64,1,2,2,128]{4,1,3,2,0:T(1,128)S(1)} fusion(f32[64,128,1,1,1]{1,2,4,3,0:T(1,128)S(1)} %bitcast.62, bf16[64,2,2,128,128]{4,3,2,1,0:T(8,128)(2,1)} %param.8), kind=kOutput, calls=%fused_computation.94 | convolution fusion | flops 50331648 | bytes 8552448 | tf_op jit(solution)/shard_map/pt,pchtd->pchd/dot_general | solution.py:26
  40.7 0.1 divide_convert_fusion
  40.8 6.8 %select_bitcast_fusion = bf16[64,2,2,128,128]{4,3,2,1,0:T(8,128)(2,1)} fusion(pred[64,128]{1,0:T(8,128)(4,1)S(1)} %iota_compare_fusion.4, bf16[64,2,2,128,128]{4,3,2,1,0:T(8,128)(2,1)} %param.8, bf16[64,2,2,128]{3,2,1,0:T(2,128)(2,1)S(1)} %divide_convert_fusion, s32[64,128]{1,0:T(8,128)S(1)} %get-tuple-element.21, pred[64,128]{1,0:T(8,128)(4,1)S(1)} %get-tuple-element.13), kind=kOutput, calls=%fused_computation.7 | convolution fusion | flops 1084227584 | bytes 16891904 | tf_op jit(solution)/shard_map/pst,pchtd->pchsd/dot_general | solution.py:21
  47.7 8.9 %gather_fusion.4 = bf16[64,2,2,128,128]{4,3,2,1,0:T(8,128)(2,1)} fusion(bf16[64,2,2,128,128]{4,3,2,1,0:T(8,128)(2,1)} %select_bitcast_fusion, s32[1024]{0:T(1024)S(1)} %pad_clamp_fusion.1), kind=kCustom, calls=%fused_computation.4 | custom fusion | bytes 16777472 | tf_op jit(solution)/shard_map/gather | solution.py:104
  56.6 7.6 %all-to-all-start.1 = ((bf16[64,2,2,128,128]{4,3,2,1,0:T(8,128)(2,1)}), bf16[64,2,2,128,128]{4,3,2,1,0:T(8,128)(2,1)}, u32[]{:S(2)}, u32[]{:S(2)}) async-start(bf16[64,2,2,128,128]{4,3,2,1,0:T(8,128)(2,1)} %gather_fusion.4), calls=%async_computation.1 | async-start | bytes 16777216 | tf_op jit(solution)/shard_map/all_to_all | solution.py:104
  64.2 0.2 reduce-scatter.2.cloned.1.call-start
  64.4 0.1 reshape.198
  64.7 0.1 fusion.15
  64.8 0.7 gather_fusion.3
  65.5 98.4 %all-to-all-done.1 = bf16[64,2,2,128,128]{4,3,2,1,0:T(8,128)(2,1)} async-done(((bf16[64,2,2,128,128]{4,3,2,1,0:T(8,128)(2,1)}), bf16[64,2,2,128,128]{4,3,2,1,0:T(8,128)(2,1)}, u32[]{:S(2)}, u32[]{:S(2)}) %all-to-all-start.1) | async-done | bytes 8388640 | tf_op jit(solution)/shard_map/all_to_all | solution.py:104
  163.9 8.9 %gather_fusion.5 = bf16[64,2,2,128,128]{4,3,2,1,0:T(8,128)(2,1)} fusion(bf16[64,2,2,128,128]{4,3,2,1,0:T(8,128)(2,1)} %all-to-all-done.1, s32[1024]{0:T(1024)S(1)} %pad_clamp_fusion), kind=kCustom, calls=%fused_computation.5 | custom fusion | bytes 16777472 | tf_op jit(solution)/shard_map/gather | solution.py:108
  172.9 4.6 %select_reduce_fusion = (f32[64,2,2]{2,1,0:T(2,128)S(1)}, f32[64,2,128,2]{2,3,1,0:T(2,128)S(1)}) fusion(pred[64,128]{1,0:T(8,128)(4,1)S(1)} %broadcast_compare_fusion, bf16[64,2,2,128]{3,2,1,0:T(2,128)(2,1)S(1)} %bitcast.63, bf16[64,2,2,128,128]{4,3,2,1,0:T(8,128)(2,1)} %gather_fusion.5), kind=kOutput, calls=%fused_computation.24 | convolution fusion | flops 8486656 | bytes 4400128 | tf_op jit(solution)/shard_map/phgd,phtd->phgt/dot_general | solution.py:43
  177.5 0.4 bitcast_reduce_fusion
  178.1 3.5 %multiply_reduce_fusion = f32[8,2,2,128]{3,2,1,0:T(2,128)S(1)} fusion(f32[8,8,2,2]{3,2,1,0:T(2,128)S(1)} %get-tuple-element.9, bf16[64,2,2,128,128]{4,3,2,1,0:T(8,128)(2,1)} %gather_fusion.5, f32[64,2,128,2]{2,3,1,0:T(2,128)S(1)} %get-tuple-element.26, f32[64,2,2]{2,1,0:T(2,128)S(1)} %get-tuple-element.25, f32[64,128]{1,0:T(8,128)S(1)} %convert_element_type.53, ...), kind=kOutput, calls=%fused_computation.22 | convolution fusion | flops 8581120 | bytes 4384768 | tf_op jit(solution)/shard_map/phgt,phtd->phgd/dot_general | solution.py:54
  181.6 0.1 fusion.13
  181.7 1.0 convolution_convert_fusion
  182.7 20.8 %reduce-scatter.2.cloned.1.call-done = bf16[8,512]{1,0:T(8,128)(2,1)} async-done(((bf16[8,2048]{1,0:T(8,128)(2,1)}), bf16[8,512]{1,0:T(8,128)(2,1)}) %reduce-scatter.2.cloned.1.call-update) | async-done | bytes 8208 | tf_op jit(solution)/shard_map/reduce_scatter | solution.py:134
  (40 shorter events, 0.7 us)
Async XLA Ops:
  7.2 174.5 %copy-start = (bf16[512,2048]{1,0:T(8,128)(2,1)S(1)}, bf16[512,2048]{1,0:T(8,128)(2,1)}, u32[]{:S(2)}) copy-start(bf16[512,2048]{1,0:T(8,128)(2,1)} %param.15) | copy-start | bytes 6291460
  24.3 23.4 %copy-start.1 = (bf16[64,128]{1,0:T(8,128)(2,1)}, bf16[64,128]{1,0:T(8,128)(2,1)S(1)}, u32[]{:S(2)}) copy-start(bf16[64,128]{1,0:T(8,128)(2,1)S(1)} %select_convert_fusion) | copy-start | bytes 49156
  25.5 31.1 %all-to-all-start = ((bf16[32,2,128]{2,1,0:T(2,128)(2,1)}), bf16[32,2,128]{2,1,0:T(2,128)(2,1)S(1)}, u32[]{:S(2)}, u32[]{:S(2)}) async-start(bf16[32,2,128]{2,1,0:T(2,128)(2,1)} %bitcast.8), calls=%async_computation | async-start | bytes 32768 | tf_op jit(solution)/shard_map/all_to_all | solution.py:105
  56.6 8.1 %copy-start.4 = (bf16[8,2,2,128]{3,2,1,0:T(2,128)(2,1)S(1)}, bf16[8,2,2,128]{3,2,1,0:T(2,128)(2,1)}, u32[]{:S(2)}) copy-start(bf16[8,2,2,128]{3,2,1,0:T(2,128)(2,1)} %param.14) | copy-start | bytes 24580
  56.6 8.1 %copy-start.3 = (bf16[8,4,128]{2,1,0:T(4,128)(2,1)S(1)}, bf16[8,4,128]{2,1,0:T(4,128)(2,1)}, u32[]{:S(2)}) copy-start(bf16[8,4,128]{2,1,0:T(4,128)(2,1)} %param.13) | copy-start | bytes 24580
  56.6 107.3 %all-to-all-start.1 = ((bf16[64,2,2,128,128]{4,3,2,1,0:T(8,128)(2,1)}), bf16[64,2,2,128,128]{4,3,2,1,0:T(8,128)(2,1)}, u32[]{:S(2)}, u32[]{:S(2)}) async-start(bf16[64,2,2,128,128]{4,3,2,1,0:T(8,128)(2,1)} %gather_fusion.4), calls=%async_computation.1 | async-start | bytes 16777216 | tf_op jit(solution)/shard_map/all_to_all | solution.py:104
  64.2 139.4 %reduce-scatter.2.cloned.1.call-start = ((), (), s32[]{:S(2)}) async-start(), calls=%async_computation.3 | async-start | bytes 40960 | tf_op jit(solution)/shard_map/reduce_scatter | solution.py:134
  181.7 21.9 %copy-start.2 = (bf16[8,512]{1,0:T(8,128)(2,1)}, bf16[8,512]{1,0:T(8,128)(2,1)S(1)}, u32[]{:S(2)}) copy-start(bf16[8,512]{1,0:T(8,128)(2,1)S(1)} %convert_element_type.58) | copy-start | bytes 24580
Sparse Core Ops, SparseCore 0:
  182.8 20.6 reduce-scatter.1
where the time goes:
time: 212 us; the launch traced here: 210 us
  waiting for transfers between devices  119 us (56%)
  local copies, waits for them, and re-layouts  31.4 us (15%)
  matrix products  21.7 us (10%)
  starting transfers between devices  17.2 us (8%)
  between operations  14.3 us (7%)
  other arithmetic  6.46 us (3%)
    all_to_all x1, waiting for transfers between devices, per_device(): lax.all_to_all(packed[send_order], 'seq', split_axis=0, concat_axis=0, ti...  98.4 us
    reduce_scatter x1, waiting for transfers between devices, per_device(): lax.psum_scatter(partial_value.astype(jnp.bfloat16), 'kv', scatter_dimens...  20.8 us
    all_to_all x1, starting transfers between devices, per_device(): lax.all_to_all(page_mass[send_order], 'seq', split_axis=0, concat_axis=0,...  9.43 us
    gather x1, local copies, waits for them, and re-layouts, per_device(): packed[send_order]  8.9 us
    gather x1, local copies, waits for them, and re-layouts, per_device(): moved[own_rows]  8.9 us
    scatter x1, local copies, waits for them, and re-layouts, per_device(): logical = jnp.zeros((all_pages,), jnp.int32).at[table_flat].set(jnp.arang...  8.05 us
    all_to_all x1, starting transfers between devices, per_device(): lax.all_to_all(packed[send_order], 'seq', split_axis=0, concat_axis=0, ti...  7.57 us
    dot_general x1, matrix products, compact_pages(): jnp.einsum('pst,pchtd->pchsd', selector, page_cache, preferred_element_ty...  6.84 us
  transfers between devices with their start and end apart: 3, of which 2 were waited for; matrix products, arithmetic and copies ran while one was open for 11% of the time, Pallas kernels for 0%

commit v1 on v0

v1 whole, which is shorter than its diff:
```python
import functools

import jax
import jax.numpy as jnp
from jax import lax
from jax.experimental import pallas as pl
from jax.experimental.pallas import tpu as pltpu
from jax.sharding import PartitionSpec as P

MESH = pl.DeviceIdType.MESH
F32 = jnp.float32
BF16 = jnp.bfloat16
I32 = jnp.int32
floor_value = -1e30
CHUNK = 4


def iota(shape, axis):
    return lax.broadcasted_iota(I32, shape, axis)


def split(x, parts):
    out = []
    for _ in range(parts):
        piece = x.astype(BF16)
        out.append(piece)
        x = x - piece.astype(F32)
    return out


def dot(a, b):
    return jnp.dot(a, b, preferred_element_type=F32)


def dot_nt(a, b):
    return lax.dot_general(a, b, (((1,), (1,)), ((), ())), preferred_element_type=F32)


def one_hot_dot(mask, x, parts):
    sel = mask.astype(F32).astype(BF16)
    return sum(dot(sel, piece) for piece in split(x, parts))


def to_row(col, diag):
    return jnp.sum(jnp.where(diag, col, 0.0), axis=0, keepdims=True)


def main_kernel(
    page_hbm, keep_hbm, weight_hbm, table_hbm, lengths_hbm, query_hbm, fresh_hbm, out_weight_hbm,
    packed_ref, mass_ref, attended_ref, projected_ref,
    pages, keep, weight, table, lengths, query, fresh, out_weight,
    query_flat, fresh_flat, query_send, query_recv, part_send, part_recv, sum_send, sum_recv,
    target_rows, count_rows, fold_rows, divisor_rows, mass_rows, query_rows, score_rows, stat_rows, part_rows,
    page_sem, in_sem, query_sems, part_sems, sum_sems,
):
    kv_count, seq_count = lax.axis_size("kv"), lax.axis_size("seq")
    kv_me, me = lax.axis_index("kv"), lax.axis_index("seq")

    def page_copy(i):
        return pltpu.make_async_copy(
            page_hbm.at[pl.ds(i * CHUNK, CHUNK)], pages.at[pl.ds(i * CHUNK, CHUNK)], page_sem.at[i]
        )

    small = [
        pltpu.make_async_copy(src, dst, in_sem.at[i])
        for i, (src, dst) in enumerate(
            [(table_hbm, table), (query_hbm, query), (lengths_hbm, lengths), (keep_hbm, keep),
             (weight_hbm, weight), (fresh_hbm, fresh), (out_weight_hbm, out_weight)]
        )
    ]
    for copy in small[:6]:
        copy.start()

    barrier = pltpu.get_barrier_semaphore()

    @pl.loop(1, seq_count)
    def _(k):
        pl.semaphore_signal(
            barrier, inc=1, device_id=(kv_me, lax.rem(me + k, seq_count)), device_id_type=MESH
        )

    @pl.loop(1, kv_count)
    def _(k):
        pl.semaphore_signal(
            barrier, inc=1, device_id=(lax.rem(kv_me + k, kv_count), me), device_id_type=MESH
        )

    @pl.loop(0, 64 // CHUNK)
    def _(i):
        page_copy(i).start()

    small[6].start()

    def exchange(send, recv, sems, rows):
        def one(k):
            other = lax.rem(me + k, seq_count)
            return pltpu.make_async_remote_copy(
                src_ref=send.at[other, pl.ds(0, rows)],
                dst_ref=recv.at[me, pl.ds(0, rows)],
                send_sem=sems.at[0],
                recv_sem=sems.at[1],
                device_id=(kv_me, other),
                device_id_type=MESH,
            )

        def every():
            return pltpu.make_async_remote_copy(
                src_ref=send.at[pl.ds(0, seq_count - 1), pl.ds(0, rows)],
                dst_ref=recv.at[pl.ds(0, seq_count - 1), pl.ds(0, rows)],
                send_sem=sems.at[0],
                recv_sem=sems.at[1],
                device_id=(kv_me, me),
                device_id_type=MESH,
            )

        def start():
            pl.loop(1, seq_count)(lambda k: one(k).start())
            recv[me] = send[me]

        return start, every()

    small[0].wait()
    small[1].wait()
    table_t = table[...]
    for r in range(8):
        query_flat[pl.ds(4 * r, 4), :] = query[r].astype(F32)

    lane = iota((64, 128), 1)
    row = iota((64, 128), 0)
    diag = lane == row
    own_pick = (iota((256, 128), 0) == 8 * me + (iota((256, 128), 1) & 7)).astype(F32).astype(BF16)
    keep_lane = (iota((8, 128), 1) >> 3) == iota((8, 128), 0)

    def own_row(x):
        y = dot(x.astype(F32).astype(BF16), own_pick)
        return jnp.sum(jnp.where(keep_lane, y, 0.0), axis=0, keepdims=True)

    holder_row = own_row(table_t >> 6)
    slot_row = own_row(table_t & 63)
    inside = iota((1, 128), 1) < 64
    holder_row = jnp.where(inside, holder_row, -1.0)
    page_row = holder_row * 64.0 + slot_row

    def to_col(x):
        return jnp.sum(jnp.where(diag, x, 0.0), axis=1, keepdims=True)

    earlier = jnp.logical_and(to_col(holder_row) == holder_row, to_col(page_row) < page_row)
    within_row = jnp.sum(earlier.astype(F32), axis=0, keepdims=True)
    entry_row = 2.0 * holder_row + within_row
    slot_of = 2 * (row & 31) + (row >> 5)
    entry_pick = jnp.where(inside, entry_row, -1.0) == slot_of.astype(F32)
    picked = dot(
        entry_pick.astype(F32).astype(BF16),
        jnp.concatenate(
            [
                jnp.concatenate([query_flat[pl.ds(h, 8, stride=4), :].astype(BF16).astype(F32)] * 16, axis=0)
                for h in range(4)
            ],
            axis=1,
        ).astype(BF16),
    )
    for k in range(2):
        for h in range(4):
            query_send.reshape(256, 128)[pl.ds(k * 4 + h, 32, stride=8), :] = picked[
                k * 32 : k * 32 + 32, h * 128 : h * 128 + 128
            ]

    pl.semaphore_wait(barrier, seq_count - 1 + kv_count - 1)
    start_queries, all_queries = exchange(query_send, query_recv, query_sems, 8)
    start_queries()

    small[2].wait()
    lengths_row = jnp.concatenate([lengths[0:1, :], lengths[1:2, :]], axis=1)
    number = iota((8, 256), 0)
    request = iota((8, 256), 1)
    codes = (
        jnp.clip(lengths_row - 128 * number, 0, 128) + 256 * (request >> 3) + 8192 * (request & 7)
    ).astype(F32)
    here = iota((64, 256), 0) + 64 * me
    code = jnp.zeros((64, 256), F32)
    for j in range(8):
        code = code + jnp.where(table_t[j : j + 1, :] == here, codes[j : j + 1, :], 0.0)
    code = jnp.sum(code, axis=1, keepdims=True).astype(I32)
    valid_count = code & 255
    owner = (code >> 8) & 31
    request_col = (code >> 13).astype(F32)
    owner_col = owner.astype(F32)
    owner_row = jnp.where(inside, to_row(owner_col, diag), -1.0)
    same = owner_col == owner_row
    rank_row = jnp.sum(jnp.logical_and(same, row < lane).astype(F32), axis=0, keepdims=True)
    rank_col = jnp.sum(jnp.logical_and(same, lane < row).astype(F32), axis=1, keepdims=True)
    slot_page_row = jnp.where(inside, 2.0 * owner_row + rank_row, -1.0)
    slot_page_col = 2.0 * owner_col + rank_col

    small[3].wait()
    small[4].wait()
    valid = lane < valid_count
    kept = jnp.logical_and(valid, keep[...] > 0)
    dropped = jnp.logical_and(valid, keep[...] == 0)
    kept_flag = kept.astype(F32)
    upper = (iota((128, 128), 0) < iota((128, 128), 1)).astype(F32).astype(BF16)
    position = dot(kept_flag.astype(BF16), upper)
    count = jnp.sum(kept_flag, axis=1, keepdims=True)
    dropped_weight = jnp.where(dropped, weight[...], 0.0)
    weight_sum = jnp.sum(dropped_weight, axis=1, keepdims=True)
    target_rows[...] = jnp.where(kept, position, -1.0)
    count_rows[...] = jnp.broadcast_to(count, (64, 128))
    divisor_rows[...] = jnp.broadcast_to(jnp.maximum(weight_sum, 1.0), (64, 128))
    for i, piece in enumerate(split(dropped_weight, 3)):
        fold_rows[i] = piece.astype(F32)
    lane_f = lane.astype(F32)
    mass = jnp.where(lane_f < count, 1.0, jnp.where(lane_f == count, weight_sum, 0.0)).astype(BF16)
    mass_ref[...] = mass
    mass_rows[...] = mass.astype(F32)

    slots = iota((128, 128), 0).astype(F32)
    extra_row = iota((16, 128), 0)

    def compact(p):
        target = target_rows[pl.ds(p, 1), :]
        picks = jnp.where(slots == target, 1.0, 0.0)
        extra = jnp.where(extra_row == 0, fold_rows[0, pl.ds(p, 1), :], 0.0)
        extra = jnp.where(extra_row == 1, fold_rows[1, pl.ds(p, 1), :], extra)
        extra = jnp.where(extra_row == 2, fold_rows[2, pl.ds(p, 1), :], extra)
        lhs = jnp.concatenate([picks.astype(BF16), extra.astype(BF16)], axis=0)
        page = jnp.concatenate(
            [pages[p, 0, 0], pages[p, 0, 1], pages[p, 1, 0], pages[p, 1, 1]], axis=1
        )
        moved = dot(lhs, page)
        divisor = divisor_rows[pl.ds(p, 1), :]
        folded = jnp.sum(moved[128:136, :], axis=0, keepdims=True)
        at_fold = slots == count_rows[pl.ds(p, 1), :]
        for i in range(4):
            cols = slice(128 * i, 128 * i + 128)
            packed_ref[p, i // 2, i % 2] = jnp.where(
                at_fold, folded[:, cols] / divisor, moved[:128, cols]
            ).astype(BF16)

    @pl.loop(0, 64 // CHUNK)
    def _(i):
        page_copy(i).wait()
        for j in range(CHUNK):
            compact(i * CHUNK + j)

    all_queries.wait_recv()
    query_recv_flat = query_recv.reshape(256, 128)
    page_pick = slot_page_col == (2 * (lane & 31) + (lane >> 5)).astype(F32)
    page_pick = jnp.logical_and(page_pick, lane < 64).astype(F32).astype(BF16)
    sent = jnp.concatenate(
        [
            jnp.concatenate(
                [query_recv_flat[pl.ds(k * 4 + h, 32, stride=8), :] for k in (0, 1, 0, 1)], axis=0
            )
            for h in range(4)
        ],
        axis=1,
    ).astype(BF16)
    page_query = dot(page_pick, sent)
    zeros = jnp.zeros((64, 128), F32)
    for h in range(4):
        for g in range(2):
            query_rows[g, pl.ds(h, 64, stride=8), :] = (
                page_query[:, h * 128 : h * 128 + 128] if g == h // 2 else zeros
            )
            query_rows[g, pl.ds(4 + h, 64, stride=8), :] = zeros

    score_scale = 128 ** -0.5

    @pl.loop(0, 64 // CHUNK)
    def _(i):
        for j in range(CHUNK):
            p = i * CHUNK + j
            keys = jnp.concatenate([packed_ref[p, 0, 0], packed_ref[p, 0, 1]], axis=1)
            q = jnp.concatenate(
                [query_rows[g, pl.ds(pl.multiple_of(p * 8, 8), 8), :] for g in range(2)], axis=1
            ).astype(BF16)
            score_rows[p] = dot_nt(q, keys) * score_scale

    low = iota((8, 128), 0) < 2
    half = iota((8, 128), 1) < 64

    @pl.loop(0, 64 // CHUNK)
    def _(i):
        for j in range(CHUNK):
            p = i * CHUNK + j
            score = score_rows[p]
            page_mass = mass_rows[pl.ds(p, 1), :]
            live = page_mass > 0.0
            top = jnp.max(jnp.where(live, score, floor_value), axis=1, keepdims=True)
            w = jnp.where(live, page_mass * jnp.exp(score - top), 0.0)
            total = jnp.sum(w, axis=1, keepdims=True)
            stat_rows[pl.ds(pl.multiple_of(p * 8, 8), 8), :] = jnp.where(half, top, total)
            values = jnp.concatenate([packed_ref[p, 1, 0], packed_ref[p, 1, 1]], axis=1)
            part = dot(w.astype(BF16), values)
            part_rows[pl.ds(pl.multiple_of(p * 8, 8), 8), :] = jnp.where(low, part[:, :128], part[:, 128:])

    back = slot_page_row == slot_of.astype(F32)
    back = back[:, :64]
    parts = one_hot_dot(
        back, jnp.concatenate([part_rows[pl.ds(h, 64, stride=8), :] for h in range(4)], axis=1), 2
    )
    stats = jnp.where(lane == 8, request_col, 0.0)
    for h in range(4):
        stats = jnp.where((lane & 63) == h, stat_rows[pl.ds(h, 64, stride=8), :], stats)
    stats = one_hot_dot(back, stats, 3)
    part_send_flat = part_send.reshape(512, 128)
    for k in range(2):
        rows = slice(k * 32, k * 32 + 32)
        for h in range(4):
            part_send_flat[pl.ds(k * 4 + h, 32, stride=16), :] = parts[rows, h * 128 : h * 128 + 128]
        part_send_flat[pl.ds(8 + k, 32, stride=16), :] = stats[rows, :]
    start_parts, all_parts = exchange(part_send, part_recv, part_sems, 10)
    start_parts()

    small[5].wait()
    for r in range(8):
        for c in range(2):
            both = fresh[r, c].astype(F32)
            for g in range(2):
                fresh_flat[pl.ds((c * 2 + g) * 8 + r, 1), :] = both[g : g + 1, :]
    lane8 = iota((8, 128), 1)
    own = jnp.zeros((8, 128), F32)
    for h in range(4):
        q = query_flat[pl.ds(h, 8, stride=4), :]
        key = fresh_flat[pl.ds((h // 2) * 8, 8), :]
        own = jnp.where(lane8 == h, jnp.sum(q * key, axis=1, keepdims=True) * score_scale, own)

    all_queries.wait_send()
    all_parts.wait_recv()
    part_recv_flat = part_recv.reshape(512, 128)
    stats = jnp.concatenate(
        [part_recv_flat[pl.ds(8 + k, 32, stride=16), :] for k in range(2)], axis=0
    )
    request_col = jnp.sum(jnp.where(lane == 8, stats, 0.0), axis=1, keepdims=True)
    top = jnp.where(lane < 4, stats, 0.0)
    total = jnp.where(lane < 4, pltpu.roll(stats, 64, 1), 0.0)
    best = own
    for r in range(8):
        one = jnp.max(jnp.where(request_col == float(r), top, floor_value), axis=0, keepdims=True)
        best = jnp.where(jnp.logical_and(iota((8, 128), 0) == r, lane8 < 4), jnp.maximum(best, one), best)
    best_rows = jnp.zeros((64, 128), F32)
    for r in range(8):
        best_rows = jnp.where(request_col == float(r), best[r : r + 1, :], best_rows)
    factor = jnp.exp(top - best_rows)
    gather = iota((8, 128), 0).astype(F32) == jnp.where(inside, to_row(request_col, diag), -1.0)
    scaled = [
        factor[:, h : h + 1]
        * jnp.concatenate(
            [part_recv_flat[pl.ds(k * 4 + h, 32, stride=16), :] for k in range(2)], axis=0
        )
        for h in range(4)
    ]
    sums = one_hot_dot(gather[:, :64], jnp.concatenate(scaled + [factor * total], axis=1), 3)
    own_factor = jnp.exp(own - best)
    denominator = sums[:, 512:] + own_factor
    attended = jnp.concatenate(
        [
            (
                sums[:, h * 128 : h * 128 + 128]
                + own_factor[:, h : h + 1] * fresh_flat[pl.ds(16 + (h // 2) * 8, 8), :]
            )
            / denominator[:, h : h + 1]
            for h in range(4)
        ],
        axis=1,
    ).astype(BF16)
    attended_ref[...] = attended

    small[6].wait()
    for c in range(4):
        sum_send[c] = dot(attended, out_weight[:, c * 512 : c * 512 + 512])

    def sum_copy(k):
        other = lax.rem(kv_me + k, kv_count)
        return pltpu.make_async_remote_copy(
            src_ref=sum_send.at[other],
            dst_ref=sum_recv.at[kv_me],
            send_sem=sum_sems.at[0],
            recv_sem=sum_sems.at[1],
            device_id=(other, me),
            device_id_type=MESH,
        )

    pl.loop(1, kv_count)(lambda k: sum_copy(k).start())
    sum_recv[kv_me] = sum_send[kv_me]
    all_sums = pltpu.make_async_remote_copy(
        src_ref=sum_send.at[pl.ds(0, 3)],
        dst_ref=sum_recv.at[pl.ds(0, 3)],
        send_sem=sum_sems.at[0],
        recv_sem=sum_sems.at[1],
        device_id=(kv_me, me),
        device_id_type=MESH,
    )
    all_parts.wait_send()
    all_sums.wait_recv()
    projected_ref[...] = (sum_recv[0] + sum_recv[1] + sum_recv[2] + sum_recv[3]).astype(BF16)
    all_sums.wait_send()


def write_kernel(*refs):
    n = (len(refs) - 1) // 2
    copies = [pltpu.make_async_copy(refs[i], refs[n + i], refs[-1].at[i]) for i in range(n)]
    for copy in copies:
        copy.start()
    for copy in copies:
        copy.wait()


def per_device(
    page_cache, keep_list, fold_weight, page_table, lengths, queries, fresh_entries, out_weight
):
    anywhere = pl.BlockSpec(memory_space=pl.ANY)
    shapes = [((64, 2, 2, 128, 128), BF16), ((64, 128), BF16), ((8, 512), BF16), ((8, 512), BF16)]
    results = pl.pallas_call(
        main_kernel,
        out_shape=[pltpu.VMEM(shape, dtype) for shape, dtype in shapes],
        in_specs=[anywhere] * 8,
        out_specs=[pl.BlockSpec(memory_space=pltpu.VMEM)] * 4,
        scratch_shapes=[
            pltpu.VMEM((64, 2, 2, 128, 128), BF16),
            pltpu.VMEM((64, 128), I32),
            pltpu.VMEM((64, 128), F32),
            pltpu.VMEM((8, 256), I32),
            pltpu.VMEM((2, 128), I32),
            pltpu.VMEM((8, 4, 128), BF16),
            pltpu.VMEM((8, 2, 2, 128), BF16),
            pltpu.VMEM((512, 2048), BF16),
            pltpu.VMEM((32, 128), F32),
            pltpu.VMEM((32, 128), F32),
            pltpu.VMEM((32, 8, 128), F32),
            pltpu.VMEM((32, 8, 128), F32),
            pltpu.VMEM((32, 16, 128), F32),
            pltpu.VMEM((32, 16, 128), F32),
            pltpu.VMEM((4, 8, 512), F32),
            pltpu.VMEM((4, 8, 512), F32),
            pltpu.VMEM((64, 128), F32),
            pltpu.VMEM((64, 128), F32),
            pltpu.VMEM((3, 64, 128), F32),
            pltpu.VMEM((64, 128), F32),
            pltpu.VMEM((64, 128), F32),
            pltpu.VMEM((2, 512, 128), F32),
            pltpu.VMEM((64, 8, 128), F32),
            pltpu.VMEM((512, 128), F32),
            pltpu.VMEM((512, 128), F32),
            pltpu.SemaphoreType.DMA((64 // CHUNK,)),
            pltpu.SemaphoreType.DMA((7,)),
            pltpu.SemaphoreType.DMA((2,)),
            pltpu.SemaphoreType.DMA((2,)),
            pltpu.SemaphoreType.DMA((2,)),
        ],
        compiler_params=pltpu.CompilerParams(
            collective_id=0, has_side_effects=True, vmem_limit_bytes=36 << 20
        ),
        name="decode",
    )(
        *(
            pltpu.with_memory_space_constraint(x, pltpu.HBM)
            for x in (
                page_cache, keep_list, fold_weight, page_table.T, lengths.reshape(2, 128), queries,
                fresh_entries, out_weight,
            )
        )
    )
    return tuple(
        pl.pallas_call(
            write_kernel,
            out_shape=[jax.ShapeDtypeStruct(shape, dtype) for shape, dtype in shapes],
            in_specs=[anywhere] * 4,
            out_specs=[anywhere] * 4,
            scratch_shapes=[pltpu.SemaphoreType.DMA((4,))],
            compiler_params=pltpu.CompilerParams(vmem_limit_bytes=1 << 20),
            name="write",
        )(*results)
    )


def solution(mesh):
    placed = (
        P("seq", None, "kv", None, None),
        P("seq", None),
        P("seq", None),
        P(),
        P(),
        P("seq", "kv", None),
        P("seq", None, "kv", None),
        P("kv", None),
    )
    return jax.shard_map(
        per_device,
        mesh=mesh,
        in_specs=placed,
        out_specs=(
            P("seq", None, "kv", None, None),
            P("seq", None),
            P("seq", "kv"),
            P("seq", "kv"),
        ),
        check_vma=False,
    )
```

time: 212 us -> 34.8 us (0.16)
  waiting for transfers between devices: 119 us -> 0 us
  Pallas kernels: 0 us -> 34 us
  local copies, waits for them, and re-layouts: 31.4 us -> 0 us
  matrix products: 21.7 us -> 0 us
  starting transfers between devices: 17.2 us -> 0 us
  between operations: 14.3 us -> 0.64 us
  other arithmetic: 6.46 us -> 0 us
    all_to_all x2 -> x0, waiting for transfers between devices: 98.4 us -> none  [the longest x1 98.4 us: per_device(): lax.all_to_all(packed[send_order], 'seq', split_axis=0, concat_axis=0, ti...]
    pallas_call x0 -> x2, Pallas kernels: none -> 34 us  [the longest x1 30.6 us: per_device(): pl.pallas_call(main_kernel, out_shape=[pltpu.VMEM(shape, dtype) for shape...]
    gather x6 -> x0, local copies, waits for them, and re-layouts: 21.9 us -> none  [the longest x1 8.9 us: per_device(): packed[send_order]]
    dot_general x6 -> x0, matrix products: 21.7 us -> none  [the longest x1 6.84 us: compact_pages(): jnp.einsum('pst,pchtd->pchsd', selector, page_cache, preferred_element_ty...]
    reduce_scatter x1 -> x0, waiting for transfers between devices: 20.8 us -> none  [per_device(): lax.psum_scatter(partial_value.astype(jnp.bfloat16), 'kv', scatter_dimens...]
    all_to_all x2 -> x0, starting transfers between devices: 17 us -> none  [the longest x1 9.43 us: per_device(): lax.all_to_all(page_mass[send_order], 'seq', split_axis=0, concat_axis=0,...]
    scatter x1 -> x0, local copies, waits for them, and re-layouts: 8.05 us -> none  [per_device(): logical = jnp.zeros((all_pages,), jnp.int32).at[table_flat].set(jnp.arang...]
    reduce_sum x4 -> x0, other arithmetic: 2.41 us -> none  [the longest x1 0.96 us: compact_pages(): weight_sum = jnp.sum(dropped_weight, axis=1)]
  transfers between devices with their start and end apart: 3 -> 0, of which waited for: 2 -> 0; matrix products, arithmetic and copies ran while one was open for 11% -> 0% of each run, Pallas kernels for 0% -> 0%
where the time goes in v1:
time: 34.8 us; the launch traced here: 34.7 us
  Pallas kernels  34 us (98%)
  between operations  0.64 us (2%)
    pallas_call x1, Pallas kernels, per_device(): pl.pallas_call(main_kernel, out_shape=[pltpu.VMEM(shape, dtype) for shape...  30.6 us
    pallas_call x1, Pallas kernels, per_device(): pl.pallas_call(write_kernel, out_shape=[jax.ShapeDtypeStruct(shape, dtype...  3.44 us

profile of v1, /device:TPU:1, one launch (start us, length us, event | category | flops | bytes accessed | tf_op | source)
XLA Modules:
  0.0 34.7 jit_solution(3142311142640188484)
XLA Ops:
  0.6 30.6 %decode.1 = (bf16[64,2,2,128,128]{4,3,2,1,0:T(8,128)(2,1)S(1)}, bf16[64,128]{1,0:T(8,128)(2,1)S(1)}, bf16[8,512]{1,0:T(8,128)(2,1)S(1)}, bf16[8,512]{1,0:T(8,128)(2,1)S(1)}) custom-call(bf16[64,2,2,128,128]{4,3,2,1,0:T(8,128)(2,1)} %page_hbm.1, s32[64,128]{1,0:T(8,128)} %keep_hbm.1, f32[64,128]{1,0:T(8,128)} %weight_hbm.1, s32[8,256]{1,0:T(8,128)} %bitcast.2, ...), custom_call_target="tpu_custom_call" | custom-call | tf_op jit(solution)/shard_map/decode/pallas_call | solution.py:414
  31.2 3.4 %write.1 = (bf16[64,2,2,128,128]{4,3,2,1,0:T(8,128)(2,1)}, bf16[64,128]{1,0:T(8,128)(2,1)}, bf16[8,512]{1,0:T(8,128)(2,1)}, bf16[8,512]{1,0:T(8,128)(2,1)}) custom-call(bf16[64,2,2,128,128]{4,3,2,1,0:T(8,128)(2,1)S(1)} %get-tuple-element.8.refs_0_, bf16[64,128]{1,0:T(8,128)(2,1)S(1)} %get-tuple-element.9.refs_1_, ...), custom_call_target="tpu_custom_call" | custom-call | tf_op jit(solution)/shard_map/write/pallas_call | solution.py:465

commit v2 on v1

v2 whole, which is shorter than its diff:
```python
import functools

import jax
import jax.numpy as jnp
from jax import lax
from jax.experimental import pallas as pl
from jax.experimental.pallas import tpu as pltpu
from jax.sharding import PartitionSpec as P

MESH = pl.DeviceIdType.MESH
F32 = jnp.float32
BF16 = jnp.bfloat16
I32 = jnp.int32
floor_value = -1e30
CHUNK = 4
EARLY = 6
GROUP = 4


def iota(shape, axis):
    return lax.broadcasted_iota(I32, shape, axis)


def split(x, parts):
    out = []
    for _ in range(parts):
        piece = x.astype(BF16)
        out.append(piece)
        x = x - piece.astype(F32)
    return out


def dot(a, b):
    return jnp.dot(a, b, preferred_element_type=F32)


def dot_nt(a, b):
    return lax.dot_general(a, b, (((1,), (1,)), ((), ())), preferred_element_type=F32)


def one_hot_dot(mask, x, parts):
    sel = mask.astype(F32).astype(BF16)
    return sum(dot(sel, piece) for piece in split(x, parts))


def to_row(col, diag):
    return jnp.sum(jnp.where(diag, col, 0.0), axis=0, keepdims=True)


def main_kernel(
    page_hbm, keep_hbm, weight_hbm, table_hbm, lengths_hbm, query_hbm, fresh_hbm, out_weight_hbm,
    packed_ref, mass_ref, attended_ref, projected_ref,
    pages, keep, weight, table, lengths, query, fresh, out_weight,
    query_flat, fresh_flat, query_send, query_recv, part_send, part_recv, sum_send, sum_recv,
    target_rows, count_rows, fold_rows, divisor_rows, mass_rows, score_rows, order_vmem, order,
    page_sem, in_sem, query_send_sem, query_recv_sems, part_sems, sum_sems, order_sem,
):
    kv_count, seq_count = lax.axis_size("kv"), lax.axis_size("seq")
    kv_me, me = lax.axis_index("kv"), lax.axis_index("seq")

    def page_copy(i):
        return pltpu.make_async_copy(
            page_hbm.at[pl.ds(i * CHUNK, CHUNK)], pages.at[pl.ds(i * CHUNK, CHUNK)], page_sem.at[i]
        )

    small = [
        pltpu.make_async_copy(src, dst, in_sem.at[i])
        for i, (src, dst) in enumerate(
            [(table_hbm, table), (query_hbm, query), (lengths_hbm, lengths), (keep_hbm, keep),
             (weight_hbm, weight), (fresh_hbm, fresh), (out_weight_hbm, out_weight)]
        )
    ]
    for copy in small[:6]:
        copy.start()

    def at(k):
        return lax.rem(me + k, seq_count)

    barrier = pltpu.get_barrier_semaphore()
    for k in range(1, seq_count):
        pl.semaphore_signal(barrier, inc=1, device_id=(kv_me, at(k)), device_id_type=MESH)
    for k in range(1, kv_count):
        pl.semaphore_signal(
            barrier, inc=1, device_id=(lax.rem(kv_me + k, kv_count), me), device_id_type=MESH
        )

    @pl.loop(0, 64 // CHUNK)
    def _(i):
        page_copy(i).start()

    small[6].start()

    small[0].wait()
    small[1].wait()
    small[2].wait()
    small[3].wait()
    small[4].wait()
    table_t = table[...]
    for r in range(8):
        query_flat[pl.ds(4 * r, 4), :] = query[r].astype(F32)

    lane = iota((64, 128), 1)
    row = iota((64, 128), 0)
    diag = lane == row
    own_pick = (iota((256, 128), 0) == 8 * me + (iota((256, 128), 1) & 7)).astype(F32).astype(BF16)
    keep_lane = (iota((8, 128), 1) >> 3) == iota((8, 128), 0)

    def own_row(x):
        y = dot(x.astype(F32).astype(BF16), own_pick)
        return jnp.sum(jnp.where(keep_lane, y, 0.0), axis=0, keepdims=True)

    inside = iota((1, 128), 1) < 64
    holder_row = jnp.where(inside, own_row(table_t >> 6), -1.0)
    page_row = holder_row * 64.0 + own_row(table_t & 63)

    def to_col(x):
        return jnp.sum(jnp.where(diag, x, 0.0), axis=1, keepdims=True)

    earlier = jnp.logical_and(to_col(holder_row) == holder_row, to_col(page_row) < page_row)
    within_row = jnp.sum(earlier.astype(F32), axis=0, keepdims=True)
    entry_row = jnp.where(inside, 2.0 * holder_row + within_row, -1.0)
    slot_of = (2 * (row & 31) + (row >> 5)).astype(F32)
    entry_pick = (entry_row == slot_of).astype(F32)
    entry_pick_b = entry_pick.astype(BF16)
    picked = dot(
        entry_pick_b,
        jnp.concatenate(
            [jnp.concatenate([query_flat[pl.ds(h, 8, stride=4), :]] * 16, axis=0) for h in range(4)],
            axis=1,
        ).astype(BF16),
    )
    for k in range(2):
        for h in range(4):
            query_send.reshape(256, 128)[pl.ds(k * 4 + h, 32, stride=8), :] = picked[
                k * 32 : k * 32 + 32, h * 128 : h * 128 + 128
            ]
    request_col = jnp.sum(entry_pick * (lane & 7).astype(F32), axis=1, keepdims=True)
    request_is = ((iota((8, 128), 1) & 7) == iota((8, 128), 0)).astype(F32).astype(BF16)
    gather = dot_nt(request_is, entry_pick_b)

    lengths_row = jnp.concatenate([lengths[0:1, :], lengths[1:2, :]], axis=1)
    number = iota((8, 256), 0)
    request = iota((8, 256), 1)
    codes = (jnp.clip(lengths_row - 128 * number, 0, 128) + 256 * (request >> 3)).astype(F32)
    here = iota((64, 256), 0) + 64 * me
    code = jnp.zeros((64, 256), F32)
    for j in range(8):
        code = code + jnp.where(table_t[j : j + 1, :] == here, codes[j : j + 1, :], 0.0)
    code = jnp.sum(code, axis=1, keepdims=True).astype(I32)
    valid_count = code & 255
    owner_col = (code >> 8).astype(F32)
    owner_row = jnp.where(inside, to_row(owner_col, diag), -1.0)
    before = jnp.logical_and(owner_col == owner_row, lane < row)
    slot_col = 2.0 * owner_col + jnp.sum(before.astype(F32), axis=1, keepdims=True)
    order_row = jnp.where(slot_col == lane.astype(F32), row.astype(F32), 0.0)
    order_vmem[...] = jnp.sum(order_row, axis=0, keepdims=True).astype(I32)
    order_copy = pltpu.make_async_copy(order_vmem, order, order_sem)
    order_copy.start()

    valid = lane < valid_count
    kept = jnp.logical_and(valid, keep[...] > 0)
    dropped = jnp.logical_and(valid, keep[...] == 0)
    kept_flag = kept.astype(F32)
    upper = (iota((128, 128), 0) < iota((128, 128), 1)).astype(F32).astype(BF16)
    position = dot(kept_flag.astype(BF16), upper)
    count = jnp.sum(kept_flag, axis=1, keepdims=True)
    dropped_weight = jnp.where(dropped, weight[...], 0.0)
    weight_sum = jnp.sum(dropped_weight, axis=1, keepdims=True)
    target_rows[...] = jnp.where(kept, position, -1.0)
    count_rows[...] = jnp.broadcast_to(count, (64, 128))
    divisor_rows[...] = jnp.broadcast_to(jnp.maximum(weight_sum, 1.0), (64, 128))
    for i, piece in enumerate(split(dropped_weight, 3)):
        fold_rows[i] = piece.astype(F32)
    lane_f = lane.astype(F32)
    mass = jnp.where(lane_f < count, 1.0, jnp.where(lane_f == count, weight_sum, 0.0)).astype(BF16)
    mass_ref[...] = mass
    mass_rows[...] = mass.astype(F32)

    slots = iota((128, 128), 0).astype(F32)
    extra_row = iota((16, 128), 0)

    def compact(p):
        target = target_rows[pl.ds(p, 1), :]
        picks = jnp.where(slots == target, 1.0, 0.0)
        extra = jnp.where(extra_row == 0, fold_rows[0, pl.ds(p, 1), :], 0.0)
        extra = jnp.where(extra_row == 1, fold_rows[1, pl.ds(p, 1), :], extra)
        extra = jnp.where(extra_row == 2, fold_rows[2, pl.ds(p, 1), :], extra)
        lhs = jnp.concatenate([picks.astype(BF16), extra.astype(BF16)], axis=0)
        page = jnp.concatenate(
            [pages[p, 0, 0], pages[p, 0, 1], pages[p, 1, 0], pages[p, 1, 1]], axis=1
        )
        moved = dot(lhs, page)
        divisor = divisor_rows[pl.ds(p, 1), :]
        folded = jnp.sum(moved[128:136, :], axis=0, keepdims=True)
        at_fold = slots == count_rows[pl.ds(p, 1), :]
        for i in range(4):
            cols = slice(128 * i, 128 * i + 128)
            packed_ref[p, i // 2, i % 2] = jnp.where(
                at_fold, folded[:, cols] / divisor, moved[:128, cols]
            ).astype(BF16)

    def query_copy(k):
        other = at(k)
        return pltpu.make_async_remote_copy(
            src_ref=query_send.at[other],
            dst_ref=query_recv.at[me],
            send_sem=query_send_sem,
            recv_sem=query_recv_sems.at[me],
            device_id=(kv_me, other),
            device_id_type=MESH,
        )

    @pl.loop(0, EARLY)
    def _(i):
        page_copy(i).wait()
        for j in range(CHUNK):
            compact(i * CHUNK + j)

    pl.semaphore_wait(barrier, seq_count - 1 + kv_count - 1)
    for k in range(1, seq_count):
        query_copy(k).start()
    query_recv[me] = query_send[me]

    @pl.loop(EARLY, 64 // CHUNK)
    def _(i):
        page_copy(i).wait()
        for j in range(CHUNK):
            compact(i * CHUNK + j)

    small[5].wait()
    for r in range(8):
        for c in range(2):
            both = fresh[r, c].astype(F32)
            for g in range(2):
                fresh_flat[pl.ds((c * 2 + g) * 8 + r, 1), :] = both[g : g + 1, :]
    score_scale = 128 ** -0.5
    lane8 = iota((8, 128), 1)
    row8 = iota((8, 128), 0)
    own = jnp.zeros((8, 128), F32)
    for h in range(4):
        q = query_flat[pl.ds(h, 8, stride=4), :]
        key = fresh_flat[pl.ds((h // 2) * 8, 8), :]
        own = jnp.where(lane8 == h, jnp.sum(q * key, axis=1, keepdims=True) * score_scale, own)

    order_copy.wait()
    first = row8 < 4
    head_low = (row8 & 3) < 2

    def pages_of(o):
        return order[0, 2 * o] & 63, order[0, 2 * o + 1] & 63

    def scores(k):
        o = at(k)
        a, b = pages_of(o)
        q = query_recv[o]
        q = jnp.concatenate(
            [jnp.where(head_low, q, 0.0), jnp.where(head_low, 0.0, q)], axis=1
        ).astype(BF16)
        keys = [jnp.concatenate([packed_ref[p, 0, 0], packed_ref[p, 0, 1]], axis=1) for p in (a, b)]
        score_rows[k - 1] = jnp.where(first, dot_nt(q, keys[0]), dot_nt(q, keys[1])) * score_scale

    def finish(k):
        o = at(k)
        a, b = pages_of(o)
        page_mass = jnp.where(first, mass_rows[pl.ds(a, 1), :], mass_rows[pl.ds(b, 1), :])
        live = page_mass > 0.0
        score = score_rows[k - 1]
        top = jnp.max(jnp.where(live, score, floor_value), axis=1, keepdims=True)
        w = jnp.where(live, page_mass * jnp.exp(score - top), 0.0)
        total = jnp.sum(w, axis=1, keepdims=True)
        w = w.astype(BF16)
        values = [jnp.concatenate([packed_ref[p, 1, 0], packed_ref[p, 1, 1]], axis=1) for p in (a, b)]
        part = jnp.where(jnp.concatenate([first, first], axis=1), dot(w, values[0]), dot(w, values[1]))
        part_send[o, pl.ds(0, 8), :] = jnp.where(head_low, part[:, :128], part[:, 128:])
        stat = jnp.where(lane8 == row8, top, jnp.where(lane8 == row8 + 8, total, 0.0))
        part_send[o, pl.ds(8, 1), :] = jnp.sum(stat, axis=0, keepdims=True)

    def part_copy(k):
        other = at(k)
        return pltpu.make_async_remote_copy(
            src_ref=part_send.at[other, pl.ds(0, 9)],
            dst_ref=part_recv.at[me, pl.ds(0, 9)],
            send_sem=part_sems.at[0],
            recv_sem=part_sems.at[1],
            device_id=(kv_me, other),
            device_id_type=MESH,
        )

    def query_wait(k):
        o = at(k)
        pltpu.make_async_remote_copy(
            src_ref=query_send.at[o],
            dst_ref=query_recv.at[o],
            send_sem=query_send_sem,
            recv_sem=query_recv_sems.at[o],
            device_id=(kv_me, o),
            device_id_type=MESH,
        ).wait_recv()

    def group(i):
        return [seq_count - 1 - GROUP * i - j for j in range(GROUP)]

    last = seq_count // GROUP - 1
    for k in group(0):
        query_wait(k)
    for k in group(0):
        scores(k)

    @pl.loop(1, last)
    def _(i):
        for k in group(i):
            query_wait(k)
        for k in group(i):
            scores(k)
        for k in group(i - 1):
            finish(k)
        for k in group(i - 1):
            part_copy(k).start()

    final = group(last)[:-1]
    for k in final:
        query_wait(k)
    for k in final + [seq_count]:
        scores(k)
    for k in group(last - 1):
        finish(k)
    for k in group(last - 1):
        part_copy(k).start()
    for k in final + [seq_count]:
        finish(k)
    for k in final:
        part_copy(k).start()
    part_recv[me] = part_send[me]

    def all_of(send, recv, send_sem, recv_sem, n, *rest):
        return pltpu.make_async_remote_copy(
            src_ref=send.at[(pl.ds(0, n), *rest)],
            dst_ref=recv.at[(pl.ds(0, n), *rest)],
            send_sem=send_sem,
            recv_sem=recv_sem,
            device_id=(kv_me, me),
            device_id_type=MESH,
        )

    all_parts = all_of(
        part_send, part_recv, part_sems.at[0], part_sems.at[1], seq_count - 1, pl.ds(0, 9)
    )
    all_parts.wait_recv()
    part_recv_flat = part_recv.reshape(512, 128)
    stats = part_recv_flat[pl.ds(8, 32, stride=16), :]
    top = jnp.concatenate([stats, pltpu.roll(stats, 124, 1)], axis=0)
    total = jnp.concatenate([pltpu.roll(stats, 120, 1), pltpu.roll(stats, 116, 1)], axis=0)
    top = jnp.where(lane < 4, top, 0.0)
    total = jnp.where(lane < 4, total, 0.0)
    best = own
    for r in range(8):
        one = jnp.max(jnp.where(request_col == float(r), top, floor_value), axis=0, keepdims=True)
        best = jnp.where(jnp.logical_and(row8 == r, lane8 < 4), jnp.maximum(best, one), best)
    best_rows = jnp.zeros((64, 128), F32)
    for r in range(8):
        best_rows = jnp.where(request_col == float(r), best[r : r + 1, :], best_rows)
    factor = jnp.exp(top - best_rows)
    scaled = [
        factor[:, h : h + 1]
        * jnp.concatenate(
            [part_recv_flat[pl.ds(k * 4 + h, 32, stride=16), :] for k in range(2)], axis=0
        )
        for h in range(4)
    ]
    gather_b = gather.astype(BF16)
    sums = sum(
        dot(gather_b, piece) for piece in split(jnp.concatenate(scaled + [factor * total], axis=1), 3)
    )
    own_factor = jnp.exp(own - best)
    denominator = sums[:, 512:] + own_factor
    attended = jnp.concatenate(
        [
            (
                sums[:, h * 128 : h * 128 + 128]
                + own_factor[:, h : h + 1] * fresh_flat[pl.ds(16 + (h // 2) * 8, 8), :]
            )
            / denominator[:, h : h + 1]
            for h in range(4)
        ],
        axis=1,
    ).astype(BF16)
    attended_ref[...] = attended

    small[6].wait()

    def sum_block(k):
        other = lax.rem(kv_me + k, kv_count)
        return dot(attended, out_weight[:, pl.ds(pl.multiple_of(other * 512, 512), 512)])

    for k in (2, 1, 3):
        other = lax.rem(kv_me + k, kv_count)
        sum_send[other] = sum_block(k).astype(BF16)
        pltpu.make_async_remote_copy(
            src_ref=sum_send.at[other],
            dst_ref=sum_recv.at[k - 1],
            send_sem=sum_sems.at[0],
            recv_sem=sum_sems.at[1],
            device_id=(other, me),
            device_id_type=MESH,
        ).start()
    mine = sum_block(0)
    all_parts.wait_send()
    all_of(query_send, query_recv, query_send_sem, query_recv_sems.at[0], seq_count - 1).wait_send()
    all_sums = all_of(sum_send, sum_recv, sum_sems.at[0], sum_sems.at[1], kv_count - 1)
    all_sums.wait_recv()
    for k in range(3):
        mine = mine + sum_recv[k].astype(F32)
    projected_ref[...] = mine.astype(BF16)
    all_sums.wait_send()


def write_kernel(*refs):
    n = (len(refs) - 1) // 2
    sems = refs[-1]
    copies = [
        pltpu.make_async_copy(
            refs[0].at[pl.ds(i * 8, 8)], refs[n].at[pl.ds(i * 8, 8)], sems.at[n + i]
        )
        for i in range(8)
    ] + [pltpu.make_async_copy(refs[i], refs[n + i], sems.at[i]) for i in range(1, n)]
    for copy in copies:
        copy.start()
    for copy in copies:
        copy.wait()


def per_device(
    page_cache, keep_list, fold_weight, page_table, lengths, queries, fresh_entries, out_weight
):
    anywhere = pl.BlockSpec(memory_space=pl.ANY)
    shapes = [((64, 2, 2, 128, 128), BF16), ((64, 128), BF16), ((8, 512), BF16), ((8, 512), BF16)]
    results = pl.pallas_call(
        main_kernel,
        out_shape=[pltpu.VMEM(shape, dtype) for shape, dtype in shapes],
        in_specs=[anywhere] * 8,
        out_specs=[pl.BlockSpec(memory_space=pltpu.VMEM)] * 4,
        scratch_shapes=[
            pltpu.VMEM((64, 2, 2, 128, 128), BF16),
            pltpu.VMEM((64, 128), I32),
            pltpu.VMEM((64, 128), F32),
            pltpu.VMEM((8, 256), I32),
            pltpu.VMEM((2, 128), I32),
            pltpu.VMEM((8, 4, 128), BF16),
            pltpu.VMEM((8, 2, 2, 128), BF16),
            pltpu.VMEM((512, 2048), BF16),
            pltpu.VMEM((32, 128), F32),
            pltpu.VMEM((32, 128), F32),
            pltpu.VMEM((32, 8, 128), F32),
            pltpu.VMEM((32, 8, 128), F32),
            pltpu.VMEM((32, 16, 128), F32),
            pltpu.VMEM((32, 16, 128), F32),
            pltpu.VMEM((4, 8, 512), BF16),
            pltpu.VMEM((4, 8, 512), BF16),
            pltpu.VMEM((64, 128), F32),
            pltpu.VMEM((64, 128), F32),
            pltpu.VMEM((3, 64, 128), F32),
            pltpu.VMEM((64, 128), F32),
            pltpu.VMEM((64, 128), F32),
            pltpu.VMEM((32, 8, 128), F32),
            pltpu.VMEM((1, 128), I32),
            pltpu.SMEM((1, 128), I32),
            pltpu.SemaphoreType.DMA((64 // CHUNK,)),
            pltpu.SemaphoreType.DMA((7,)),
            pltpu.SemaphoreType.DMA,
            pltpu.SemaphoreType.DMA((32,)),
            pltpu.SemaphoreType.DMA((2,)),
            pltpu.SemaphoreType.DMA((2,)),
            pltpu.SemaphoreType.DMA,
        ],
        compiler_params=pltpu.CompilerParams(
            collective_id=0, has_side_effects=True, vmem_limit_bytes=36 << 20
        ),
        name="decode",
    )(
        *(
            pltpu.with_memory_space_constraint(x, pltpu.HBM)
            for x in (
                page_cache, keep_list, fold_weight, page_table.T, lengths.reshape(2, 128), queries,
                fresh_entries, out_weight,
            )
        )
    )
    return tuple(
        pl.pallas_call(
            write_kernel,
            out_shape=[jax.ShapeDtypeStruct(shape, dtype) for shape, dtype in shapes],
            in_specs=[anywhere] * 4,
            out_specs=[anywhere] * 4,
            scratch_shapes=[pltpu.SemaphoreType.DMA((12,))],
            compiler_params=pltpu.CompilerParams(vmem_limit_bytes=1 << 20),
            name="write",
        )(*results)
    )


def solution(mesh):
    placed = (
        P("seq", None, "kv", None, None),
        P("seq", None),
        P("seq", None),
        P(),
        P(),
        P("seq", "kv", None),
        P("seq", None, "kv", None),
        P("kv", None),
    )
    return jax.shard_map(
        per_device,
        mesh=mesh,
        in_specs=placed,
        out_specs=(
            P("seq", None, "kv", None, None),
            P("seq", None),
            P("seq", "kv"),
            P("seq", "kv"),
        ),
        check_vma=False,
    )
```

time: 34.8 us -> 29.6 us (0.85)
  Pallas kernels: 34 us -> 28.8 us
    pallas_call x1, Pallas kernels: 30.6 us -> 25.4 us  [per_device(): pl.pallas_call(main_kernel, out_shape=[pltpu.VMEM(shape, dtype) for shape...]
where the time goes in v2:
time: 29.6 us; the launch traced here: 29.5 us
  Pallas kernels  28.8 us (97%)
  between operations  0.64 us (2%)
    pallas_call x1, Pallas kernels, per_device(): pl.pallas_call(main_kernel, out_shape=[pltpu.VMEM(shape, dtype) for shape...  25.4 us
    pallas_call x1, Pallas kernels, per_device(): pl.pallas_call(write_kernel, out_shape=[jax.ShapeDtypeStruct(shape, dtype...  3.41 us

profile of v2, /device:TPU:1, one launch (start us, length us, event | category | flops | bytes accessed | tf_op | source)
XLA Modules:
  0.0 29.5 jit_solution(8727840580494744416)
XLA Ops:
  0.6 25.4 %decode.1 = (bf16[64,2,2,128,128]{4,3,2,1,0:T(8,128)(2,1)S(1)}, bf16[64,128]{1,0:T(8,128)(2,1)S(1)}, bf16[8,512]{1,0:T(8,128)(2,1)S(1)}, bf16[8,512]{1,0:T(8,128)(2,1)S(1)}) custom-call(bf16[64,2,2,128,128]{4,3,2,1,0:T(8,128)(2,1)} %page_hbm.1, s32[64,128]{1,0:T(8,128)} %keep_hbm.1, f32[64,128]{1,0:T(8,128)} %weight_hbm.1, s32[8,256]{1,0:T(8,128)} %bitcast.2, ...), custom_call_target="tpu_custom_call" | custom-call | tf_op jit(solution)/shard_map/decode/pallas_call | solution.py:437
  26.1 3.4 %write.1 = (bf16[64,2,2,128,128]{4,3,2,1,0:T(8,128)(2,1)}, bf16[64,128]{1,0:T(8,128)(2,1)}, bf16[8,512]{1,0:T(8,128)(2,1)}, bf16[8,512]{1,0:T(8,128)(2,1)}) custom-call(bf16[64,2,2,128,128]{4,3,2,1,0:T(8,128)(2,1)S(1)} %get-tuple-element.8.refs_0_, bf16[64,128]{1,0:T(8,128)(2,1)S(1)} %get-tuple-element.9.refs_1_, ...), custom_call_target="tpu_custom_call" | custom-call | tf_op jit(solution)/shard_map/write/pallas_call | solution.py:489

commit v3 on v2

--- a/solution.py
+++ b/solution.py
@@ -12,9 +12,8 @@
 BF16 = jnp.bfloat16
 I32 = jnp.int32
 floor_value = -1e30
-CHUNK = 4
-EARLY = 6
-GROUP = 4
+CHUNK = 16
+GROUP = 16
 
 
 def iota(shape, axis):
@@ -70,8 +69,12 @@
              (weight_hbm, weight), (fresh_hbm, fresh), (out_weight_hbm, out_weight)]
         )
     ]
-    for copy in small[:6]:
+    for copy in small[:5]:
         copy.start()
+
+    @pl.loop(0, 64 // CHUNK)
+    def _(i):
+        page_copy(i).start()
 
     def at(k):
         return lax.rem(me + k, seq_count)
@@ -84,17 +87,11 @@
             barrier, inc=1, device_id=(lax.rem(kv_me + k, kv_count), me), device_id_type=MESH
         )
 
-    @pl.loop(0, 64 // CHUNK)
-    def _(i):
-        page_copy(i).start()
-
+    small[5].start()
     small[6].start()
 
     small[0].wait()
     small[1].wait()
-    small[2].wait()
-    small[3].wait()
-    small[4].wait()
     table_t = table[...]
     for r in range(8):
         query_flat[pl.ds(4 * r, 4), :] = query[r].astype(F32)
@@ -134,10 +131,27 @@
             query_send.reshape(256, 128)[pl.ds(k * 4 + h, 32, stride=8), :] = picked[
                 k * 32 : k * 32 + 32, h * 128 : h * 128 + 128
             ]
+    def query_copy(k):
+        other = at(k)
+        return pltpu.make_async_remote_copy(
+            src_ref=query_send.at[other],
+            dst_ref=query_recv.at[me],
+            send_sem=query_send_sem,
+            recv_sem=query_recv_sems.at[me],
+            device_id=(kv_me, other),
+            device_id_type=MESH,
+        )
+
+    pl.semaphore_wait(barrier, seq_count - 1 + kv_count - 1)
+    for k in range(1, seq_count):
+        query_copy(k).start()
+    query_recv[me] = query_send[me]
+
     request_col = jnp.sum(entry_pick * (lane & 7).astype(F32), axis=1, keepdims=True)
     request_is = ((iota((8, 128), 1) & 7) == iota((8, 128), 0)).astype(F32).astype(BF16)
     gather = dot_nt(request_is, entry_pick_b)
 
+    small[2].wait()
     lengths_row = jnp.concatenate([lengths[0:1, :], lengths[1:2, :]], axis=1)
     number = iota((8, 256), 0)
     request = iota((8, 256), 1)
@@ -157,6 +171,8 @@
     order_copy = pltpu.make_async_copy(order_vmem, order, order_sem)
     order_copy.start()
 
+    small[3].wait()
+    small[4].wait()
     valid = lane < valid_count
     kept = jnp.logical_and(valid, keep[...] > 0)
     dropped = jnp.logical_and(valid, keep[...] == 0)
@@ -199,29 +215,7 @@
                 at_fold, folded[:, cols] / divisor, moved[:128, cols]
             ).astype(BF16)
 
-    def query_copy(k):
-        other = at(k)
-        return pltpu.make_async_remote_copy(
-            src_ref=query_send.at[other],
-            dst_ref=query_recv.at[me],
-            send_sem=query_send_sem,
-            recv_sem=query_recv_sems.at[me],
-            device_id=(kv_me, other),
-            device_id_type=MESH,
-        )
-
-    @pl.loop(0, EARLY)
-    def _(i):
-        page_copy(i).wait()
-        for j in range(CHUNK):
-            compact(i * CHUNK + j)
-
-    pl.semaphore_wait(barrier, seq_count - 1 + kv_count - 1)
-    for k in range(1, seq_count):
-        query_copy(k).start()
-    query_recv[me] = query_send[me]
-
-    @pl.loop(EARLY, 64 // CHUNK)
+    @pl.loop(0, 64 // CHUNK)
     def _(i):
         page_copy(i).wait()
         for j in range(CHUNK):

time: 29.6 us -> 28.8 us (0.973)
  Pallas kernels: 28.8 us -> 27.9 us
    pallas_call x1, Pallas kernels: 25.4 us -> 24.5 us  [per_device(): pl.pallas_call(main_kernel, out_shape=[pltpu.VMEM(shape, dtype) for shape...]
where the time goes in v3:
time: 28.8 us; the launch traced here: 28.6 us
  Pallas kernels  27.9 us (97%)
  between operations  0.64 us (2%)
    pallas_call x1, Pallas kernels, per_device(): pl.pallas_call(main_kernel, out_shape=[pltpu.VMEM(shape, dtype) for shape...  24.5 us
    pallas_call x1, Pallas kernels, per_device(): pl.pallas_call(write_kernel, out_shape=[jax.ShapeDtypeStruct(shape, dtype...  3.41 us

profile of v3, /device:TPU:1, one launch (start us, length us, event | category | flops | bytes accessed | tf_op | source)
XLA Modules:
  0.0 28.6 jit_solution(17315252583494701723)
XLA Ops:
  0.6 24.5 %decode.1 = (bf16[64,2,2,128,128]{4,3,2,1,0:T(8,128)(2,1)S(1)}, bf16[64,128]{1,0:T(8,128)(2,1)S(1)}, bf16[8,512]{1,0:T(8,128)(2,1)S(1)}, bf16[8,512]{1,0:T(8,128)(2,1)S(1)}) custom-call(bf16[64,2,2,128,128]{4,3,2,1,0:T(8,128)(2,1)} %page_hbm.1, s32[64,128]{1,0:T(8,128)} %keep_hbm.1, f32[64,128]{1,0:T(8,128)} %weight_hbm.1, s32[8,256]{1,0:T(8,128)} %bitcast.2, ...), custom_call_target="tpu_custom_call" | custom-call | tf_op jit(solution)/shard_map/decode/pallas_call | solution.py:431
  25.2 3.4 %write.1 = (bf16[64,2,2,128,128]{4,3,2,1,0:T(8,128)(2,1)}, bf16[64,128]{1,0:T(8,128)(2,1)}, bf16[8,512]{1,0:T(8,128)(2,1)}, bf16[8,512]{1,0:T(8,128)(2,1)}) custom-call(bf16[64,2,2,128,128]{4,3,2,1,0:T(8,128)(2,1)S(1)} %get-tuple-element.8.refs_0_, bf16[64,128]{1,0:T(8,128)(2,1)S(1)} %get-tuple-element.9.refs_1_, ...), custom_call_target="tpu_custom_call" | custom-call | tf_op jit(solution)/shard_map/write/pallas_call | solution.py:483

commit v4 on v3

--- a/solution.py
+++ b/solution.py
@@ -13,7 +13,12 @@
 I32 = jnp.int32
 floor_value = -1e30
 CHUNK = 16
+LEAD = 32
 GROUP = 16
+PEERS = sorted(
+    ((dz, dx, dc) for dz in range(4) for dx in range(4) for dc in range(2)),
+    key=lambda d: (-min(d[0], 4 - d[0]) - min(d[1], 4 - d[1]), -d[2], d),
+)
 
 
 def iota(shape, axis):
@@ -46,112 +51,7 @@
     return jnp.sum(jnp.where(diag, col, 0.0), axis=0, keepdims=True)
 
 
-def main_kernel(
-    page_hbm, keep_hbm, weight_hbm, table_hbm, lengths_hbm, query_hbm, fresh_hbm, out_weight_hbm,
-    packed_ref, mass_ref, attended_ref, projected_ref,
-    pages, keep, weight, table, lengths, query, fresh, out_weight,
-    query_flat, fresh_flat, query_send, query_recv, part_send, part_recv, sum_send, sum_recv,
-    target_rows, count_rows, fold_rows, divisor_rows, mass_rows, score_rows, order_vmem, order,
-    page_sem, in_sem, query_send_sem, query_recv_sems, part_sems, sum_sems, order_sem,
-):
-    kv_count, seq_count = lax.axis_size("kv"), lax.axis_size("seq")
-    kv_me, me = lax.axis_index("kv"), lax.axis_index("seq")
-
-    def page_copy(i):
-        return pltpu.make_async_copy(
-            page_hbm.at[pl.ds(i * CHUNK, CHUNK)], pages.at[pl.ds(i * CHUNK, CHUNK)], page_sem.at[i]
-        )
-
-    small = [
-        pltpu.make_async_copy(src, dst, in_sem.at[i])
-        for i, (src, dst) in enumerate(
-            [(table_hbm, table), (query_hbm, query), (lengths_hbm, lengths), (keep_hbm, keep),
-             (weight_hbm, weight), (fresh_hbm, fresh), (out_weight_hbm, out_weight)]
-        )
-    ]
-    for copy in small[:5]:
-        copy.start()
-
-    @pl.loop(0, 64 // CHUNK)
-    def _(i):
-        page_copy(i).start()
-
-    def at(k):
-        return lax.rem(me + k, seq_count)
-
-    barrier = pltpu.get_barrier_semaphore()
-    for k in range(1, seq_count):
-        pl.semaphore_signal(barrier, inc=1, device_id=(kv_me, at(k)), device_id_type=MESH)
-    for k in range(1, kv_count):
-        pl.semaphore_signal(
-            barrier, inc=1, device_id=(lax.rem(kv_me + k, kv_count), me), device_id_type=MESH
-        )
-
-    small[5].start()
-    small[6].start()
-
-    small[0].wait()
-    small[1].wait()
-    table_t = table[...]
-    for r in range(8):
-        query_flat[pl.ds(4 * r, 4), :] = query[r].astype(F32)
-
-    lane = iota((64, 128), 1)
-    row = iota((64, 128), 0)
-    diag = lane == row
-    own_pick = (iota((256, 128), 0) == 8 * me + (iota((256, 128), 1) & 7)).astype(F32).astype(BF16)
-    keep_lane = (iota((8, 128), 1) >> 3) == iota((8, 128), 0)
-
-    def own_row(x):
-        y = dot(x.astype(F32).astype(BF16), own_pick)
-        return jnp.sum(jnp.where(keep_lane, y, 0.0), axis=0, keepdims=True)
-
-    inside = iota((1, 128), 1) < 64
-    holder_row = jnp.where(inside, own_row(table_t >> 6), -1.0)
-    page_row = holder_row * 64.0 + own_row(table_t & 63)
-
-    def to_col(x):
-        return jnp.sum(jnp.where(diag, x, 0.0), axis=1, keepdims=True)
-
-    earlier = jnp.logical_and(to_col(holder_row) == holder_row, to_col(page_row) < page_row)
-    within_row = jnp.sum(earlier.astype(F32), axis=0, keepdims=True)
-    entry_row = jnp.where(inside, 2.0 * holder_row + within_row, -1.0)
-    slot_of = (2 * (row & 31) + (row >> 5)).astype(F32)
-    entry_pick = (entry_row == slot_of).astype(F32)
-    entry_pick_b = entry_pick.astype(BF16)
-    picked = dot(
-        entry_pick_b,
-        jnp.concatenate(
-            [jnp.concatenate([query_flat[pl.ds(h, 8, stride=4), :]] * 16, axis=0) for h in range(4)],
-            axis=1,
-        ).astype(BF16),
-    )
-    for k in range(2):
-        for h in range(4):
-            query_send.reshape(256, 128)[pl.ds(k * 4 + h, 32, stride=8), :] = picked[
-                k * 32 : k * 32 + 32, h * 128 : h * 128 + 128
-            ]
-    def query_copy(k):
-        other = at(k)
-        return pltpu.make_async_remote_copy(
-            src_ref=query_send.at[other],
-            dst_ref=query_recv.at[me],
-            send_sem=query_send_sem,
-            recv_sem=query_recv_sems.at[me],
-            device_id=(kv_me, other),
-            device_id_type=MESH,
-        )
-
-    pl.semaphore_wait(barrier, seq_count - 1 + kv_count - 1)
-    for k in range(1, seq_count):
-        query_copy(k).start()
-    query_recv[me] = query_send[me]
-
-    request_col = jnp.sum(entry_pick * (lane & 7).astype(F32), axis=1, keepdims=True)
-    request_is = ((iota((8, 128), 1) & 7) == iota((8, 128), 0)).astype(F32).astype(BF16)
-    gather = dot_nt(request_is, entry_pick_b)
-
-    small[2].wait()
+def place_pages(table_t, lengths, me):
     lengths_row = jnp.concatenate([lengths[0:1, :], lengths[1:2, :]], axis=1)
     number = iota((8, 256), 0)
     request = iota((8, 256), 1)
@@ -161,18 +61,12 @@
     for j in range(8):
         code = code + jnp.where(table_t[j : j + 1, :] == here, codes[j : j + 1, :], 0.0)
     code = jnp.sum(code, axis=1, keepdims=True).astype(I32)
-    valid_count = code & 255
-    owner_col = (code >> 8).astype(F32)
-    owner_row = jnp.where(inside, to_row(owner_col, diag), -1.0)
-    before = jnp.logical_and(owner_col == owner_row, lane < row)
-    slot_col = 2.0 * owner_col + jnp.sum(before.astype(F32), axis=1, keepdims=True)
-    order_row = jnp.where(slot_col == lane.astype(F32), row.astype(F32), 0.0)
-    order_vmem[...] = jnp.sum(order_row, axis=0, keepdims=True).astype(I32)
-    order_copy = pltpu.make_async_copy(order_vmem, order, order_sem)
-    order_copy.start()
-
-    small[3].wait()
-    small[4].wait()
+    return code & 255, code >> 8
+
+
+def plan_pages(valid_count, keep, weight, rows):
+    target_rows, count_rows, divisor_rows, fold_rows = rows
+    lane = iota((64, 128), 1)
     valid = lane < valid_count
     kept = jnp.logical_and(valid, keep[...] > 0)
     dropped = jnp.logical_and(valid, keep[...] == 0)
@@ -189,37 +83,185 @@
         fold_rows[i] = piece.astype(F32)
     lane_f = lane.astype(F32)
     mass = jnp.where(lane_f < count, 1.0, jnp.where(lane_f == count, weight_sum, 0.0)).astype(BF16)
+    return mass
+
+
+def compact_page(p, pages, packed_ref, rows):
+    target_rows, count_rows, divisor_rows, fold_rows = rows
+    slots = iota((128, 128), 0).astype(F32)
+    extra_row = iota((16, 128), 0)
+    target = target_rows[pl.ds(p, 1), :]
+    picks = jnp.where(slots == target, 1.0, 0.0)
+    extra = jnp.where(extra_row == 0, fold_rows[0, pl.ds(p, 1), :], 0.0)
+    extra = jnp.where(extra_row == 1, fold_rows[1, pl.ds(p, 1), :], extra)
+    extra = jnp.where(extra_row == 2, fold_rows[2, pl.ds(p, 1), :], extra)
+    lhs = jnp.concatenate([picks.astype(BF16), extra.astype(BF16)], axis=0)
+    page = jnp.concatenate(
+        [pages[p, 0, 0], pages[p, 0, 1], pages[p, 1, 0], pages[p, 1, 1]], axis=1
+    )
+    moved = dot(lhs, page)
+    divisor = divisor_rows[pl.ds(p, 1), :]
+    folded = jnp.sum(moved[128:136, :], axis=0, keepdims=True)
+    at_fold = slots == count_rows[pl.ds(p, 1), :]
+    for i in range(4):
+        cols = slice(128 * i, 128 * i + 128)
+        packed_ref[p, i // 2, i % 2] = jnp.where(
+            at_fold, folded[:, cols] / divisor, moved[:128, cols]
+        ).astype(BF16)
+
+
+def share():
+    kv_me, me = lax.axis_index("kv"), lax.axis_index("seq")
+
+    def pick(i, values):
+        out = values[-1]
+        for at in range(len(values) - 1):
+            out = jnp.where(i == at, values[at], out)
+        return out
+
+    lead = (
+        pick(kv_me, (0, 11, 18, 21))
+        + pick(me // 8, (0, 13, 27, 29))
+        + pick(lax.rem(me // 2, 4), (0, 9, 13, 12))
+        + 8 * lax.rem(me, 2)
+    )
+    return jnp.clip((LEAD - lead + 3) // 4, 0, 8)
+
+
+def main_kernel(
+    page_hbm, keep_hbm, weight_hbm, table_hbm, lengths_hbm, query_hbm, fresh_hbm, out_weight_hbm,
+    early,
+    packed_ref, mass_ref, attended_ref, projected_ref,
+    pages, keep, weight, table, lengths, query, fresh, out_weight,
+    query_flat, fresh_flat, query_send, query_recv, part_send, part_recv, sum_send, sum_recv,
+    target_rows, count_rows, fold_rows, divisor_rows, mass_rows, score_rows, order_vmem, order,
+    page_sem, in_sem, query_send_sem, query_recv_sems, part_sems, sum_sems, order_sem,
+):
+    kv_count, seq_count = lax.axis_size("kv"), lax.axis_size("seq")
+    kv_me, me = lax.axis_index("kv"), lax.axis_index("seq")
+
+    def page_copy(i):
+        return pltpu.make_async_copy(
+            page_hbm.at[pl.ds(i * CHUNK, CHUNK)], pages.at[pl.ds(i * CHUNK, CHUNK)], page_sem.at[i]
+        )
+
+    small = [
+        pltpu.make_async_copy(src, dst, in_sem.at[i])
+        for i, (src, dst) in enumerate(
+            [(table_hbm, table), (query_hbm, query), (lengths_hbm, lengths), (keep_hbm, keep),
+             (weight_hbm, weight), (fresh_hbm, fresh), (out_weight_hbm, out_weight)]
+        )
+    ]
+    for copy in small[:5]:
+        copy.start()
+
+    @pl.loop(0, 64 // CHUNK)
+    def _(i):
+        page_copy(i).start()
+
+    where_z, where_x, where_core = me // 8, lax.rem(me // 2, 4), lax.rem(me, 2)
+
+    def at(k):
+        dz, dx, dc = PEERS[k - 1]
+        return (
+            lax.rem(where_z + dz, 4) * 8 + lax.rem(where_x + dx, 4) * 2 + lax.rem(where_core + dc, 2)
+        )
+
+    barrier = pltpu.get_barrier_semaphore()
+    for k in range(1, seq_count):
+        pl.semaphore_signal(barrier, inc=1, device_id=(kv_me, at(k)), device_id_type=MESH)
+    for k in range(1, kv_count):
+        pl.semaphore_signal(
+            barrier, inc=1, device_id=(lax.rem(kv_me + k, kv_count), me), device_id_type=MESH
+        )
+
+    small[5].start()
+    small[6].start()
+
+    small[0].wait()
+    small[1].wait()
+    table_t = table[...]
+    for r in range(8):
+        query_flat[pl.ds(4 * r, 4), :] = query[r].astype(F32)
+
+    lane = iota((64, 128), 1)
+    row = iota((64, 128), 0)
+    diag = lane == row
+    own_pick = (iota((256, 128), 0) == 8 * me + (iota((256, 128), 1) & 7)).astype(F32).astype(BF16)
+    keep_lane = (iota((8, 128), 1) >> 3) == iota((8, 128), 0)
+
+    def own_row(x):
+        y = dot(x.astype(F32).astype(BF16), own_pick)
+        return jnp.sum(jnp.where(keep_lane, y, 0.0), axis=0, keepdims=True)
+
+    inside = iota((1, 128), 1) < 64
+    holder_row = jnp.where(inside, own_row(table_t >> 6), -1.0)
+    page_row = holder_row * 64.0 + own_row(table_t & 63)
+
+    def to_col(x):
+        return jnp.sum(jnp.where(diag, x, 0.0), axis=1, keepdims=True)
+
+    earlier = jnp.logical_and(to_col(holder_row) == holder_row, to_col(page_row) < page_row)
+    within_row = jnp.sum(earlier.astype(F32), axis=0, keepdims=True)
+    entry_row = jnp.where(inside, 2.0 * holder_row + within_row, -1.0)
+    slot_of = (2 * (row & 31) + (row >> 5)).astype(F32)
+    entry_pick = (entry_row == slot_of).astype(F32)
+    entry_pick_b = entry_pick.astype(BF16)
+    picked = dot(
+        entry_pick_b,
+        jnp.concatenate(
+            [jnp.concatenate([query_flat[pl.ds(h, 8, stride=4), :]] * 16, axis=0) for h in range(4)],
+            axis=1,
+        ).astype(BF16),
+    )
+    for k in range(2):
+        for h in range(4):
+            query_send.reshape(256, 128)[pl.ds(k * 4 + h, 32, stride=8), :] = picked[
+                k * 32 : k * 32 + 32, h * 128 : h * 128 + 128
+            ]
+    def query_copy(k):
+        other = at(k)
+        return pltpu.make_async_remote_copy(
+            src_ref=query_send.at[other],
+            dst_ref=query_recv.at[me],
+            send_sem=query_send_sem,
+            recv_sem=query_recv_sems.at[me],
+            device_id=(kv_me, other),
+            device_id_type=MESH,
+        )
+
+    pl.semaphore_wait(barrier, seq_count - 1 + kv_count - 1)
+    for k in range(1, seq_count):
+        query_copy(k).start()
+    query_recv[me] = query_send[me]
+
+    request_col = jnp.sum(entry_pick * (lane & 7).astype(F32), axis=1, keepdims=True)
+    request_is = ((iota((8, 128), 1) & 7) == iota((8, 128), 0)).astype(F32).astype(BF16)
+    gather = dot_nt(request_is, entry_pick_b)
+
+    small[2].wait()
+    valid_count, owner = place_pages(table_t, lengths, me)
+    owner_col = owner.astype(F32)
+    owner_row = jnp.where(inside, to_row(owner_col, diag), -1.0)
+    before = jnp.logical_and(owner_col == owner_row, lane < row)
+    slot_col = 2.0 * owner_col + jnp.sum(before.astype(F32), axis=1, keepdims=True)
+    order_row = jnp.where(slot_col == lane.astype(F32), row.astype(F32), 0.0)
+    order_vmem[...] = jnp.sum(order_row, axis=0, keepdims=True).astype(I32)
+    order_copy = pltpu.make_async_copy(order_vmem, order, order_sem)
+    order_copy.start()
+
+    small[3].wait()
+    small[4].wait()
+    rows = (target_rows, count_rows, divisor_rows, fold_rows)
+    mass = plan_pages(valid_count, keep, weight, rows)
     mass_ref[...] = mass
     mass_rows[...] = mass.astype(F32)
-
-    slots = iota((128, 128), 0).astype(F32)
-    extra_row = iota((16, 128), 0)
-
-    def compact(p):
-        target = target_rows[pl.ds(p, 1), :]
-        picks = jnp.where(slots == target, 1.0, 0.0)
-        extra = jnp.where(extra_row == 0, fold_rows[0, pl.ds(p, 1), :], 0.0)
-        extra = jnp.where(extra_row == 1, fold_rows[1, pl.ds(p, 1), :], extra)
-        extra = jnp.where(extra_row == 2, fold_rows[2, pl.ds(p, 1), :], extra)
-        lhs = jnp.concatenate([picks.astype(BF16), extra.astype(BF16)], axis=0)
-        page = jnp.concatenate(
-            [pages[p, 0, 0], pages[p, 0, 1], pages[p, 1, 0], pages[p, 1, 1]], axis=1
-        )
-        moved = dot(lhs, page)
-        divisor = divisor_rows[pl.ds(p, 1), :]
-        folded = jnp.sum(moved[128:136, :], axis=0, keepdims=True)
-        at_fold = slots == count_rows[pl.ds(p, 1), :]
-        for i in range(4):
-            cols = slice(128 * i, 128 * i + 128)
-            packed_ref[p, i // 2, i % 2] = jnp.where(
-                at_fold, folded[:, cols] / divisor, moved[:128, cols]
-            ).astype(BF16)
 
     @pl.loop(0, 64 // CHUNK)
     def _(i):
         page_copy(i).wait()
         for j in range(CHUNK):
-            compact(i * CHUNK + j)
+            compact_page(i * CHUNK + j, pages, packed_ref, rows)
 
     small[5].wait()
     for r in range(8):
@@ -292,37 +334,22 @@
         ).wait_recv()
 
     def group(i):
-        return [seq_count - 1 - GROUP * i - j for j in range(GROUP)]
-
-    last = seq_count // GROUP - 1
-    for k in group(0):
-        query_wait(k)
-    for k in group(0):
-        scores(k)
-
-    @pl.loop(1, last)
-    def _(i):
-        for k in group(i):
+        return [GROUP * i + j + 1 for j in range(GROUP)]
+
+    for i in range(seq_count // GROUP):
+        others = [k for k in group(i) if k < seq_count]
+        for k in others:
             query_wait(k)
         for k in group(i):
             scores(k)
-        for k in group(i - 1):
-            finish(k)
-        for k in group(i - 1):
-            part_copy(k).start()
-
-    final = group(last)[:-1]
-    for k in final:
-        query_wait(k)
-    for k in final + [seq_count]:
-        scores(k)
-    for k in group(last - 1):
+        if i > 0:
+            for k in group(i - 1):
+                finish(k)
+            for k in group(i - 1):
+                part_copy(k).start()
+    for k in group(i):
         finish(k)
-    for k in group(last - 1):
-        part_copy(k).start()
-    for k in final + [seq_count]:
-        finish(k)
-    for k in final:
+    for k in others:
         part_copy(k).start()
     part_recv[me] = part_send[me]
 
@@ -408,19 +435,67 @@
     all_sums.wait_send()
 
 
-def write_kernel(*refs):
-    n = (len(refs) - 1) // 2
-    sems = refs[-1]
-    copies = [
-        pltpu.make_async_copy(
-            refs[0].at[pl.ds(i * 8, 8)], refs[n].at[pl.ds(i * 8, 8)], sems.at[n + i]
-        )
-        for i in range(8)
-    ] + [pltpu.make_async_copy(refs[i], refs[n + i], sems.at[i]) for i in range(1, n)]
-    for copy in copies:
+def early_kernel(
+    page_hbm, keep_hbm, weight_hbm, table_hbm, lengths_hbm, out_hbm,
+    pages, packed, keep, weight, table, lengths,
+    target_rows, count_rows, fold_rows, divisor_rows, page_sem, in_sem, out_sem,
+):
+    me = lax.axis_index("seq")
+    pieces = share()
+
+    def page_copy(i):
+        at = pl.ds(i * 8, 8)
+        return pltpu.make_async_copy(page_hbm.at[at], pages.at[at], page_sem.at[i])
+
+    def out_copy(i):
+        at = pl.ds(i * 8, 8)
+        return pltpu.make_async_copy(packed.at[at], out_hbm.at[at], out_sem.at[i])
+
+    @pl.when(pieces > 0)
+    def _():
+        small = [
+            pltpu.make_async_copy(src, dst, in_sem.at[i])
+            for i, (src, dst) in enumerate(
+                [(table_hbm, table), (lengths_hbm, lengths), (keep_hbm, keep), (weight_hbm, weight)]
+            )
+        ]
+        for copy in small:
+            copy.start()
+        pl.loop(0, pieces)(lambda i: page_copy(i).start())
+        for copy in small:
+            copy.wait()
+        valid_count, _ = place_pages(table[...], lengths, me)
+        rows = (target_rows, count_rows, divisor_rows, fold_rows)
+        plan_pages(valid_count, keep, weight, rows)
+
+        @pl.loop(0, pieces)
+        def _(i):
+            page_copy(i).wait()
+            for j in range(8):
+                compact_page(i * 8 + j, pages, packed, rows)
+            out_copy(i).start()
+
+        pl.loop(0, pieces)(lambda i: out_copy(i).wait())
+
+
+def write_kernel(packed, mass, attended, projected, early, *rest):
+    outs, sems = rest[:4], rest[4]
+    pieces = share()
+
+    def packed_copy(i):
+        at = pl.ds(i * 8, 8)
+        return pltpu.make_async_copy(packed.at[at], outs[0].at[at], sems.at[3 + i])
+
+    small = [
+        pltpu.make_async_copy(src, dst, sems.at[i])
+        for i, (src, dst) in enumerate(zip((mass, attended, projected), outs[1:]))
+    ]
+    pl.loop(pieces, 8)(lambda i: packed_copy(i).start())
+    for copy in small:
         copy.start()
-    for copy in copies:
+    for copy in small:
         copy.wait()
+    pl.loop(pieces, 8)(lambda i: packed_copy(i).wait())
 
 
 def per_device(
@@ -428,10 +503,40 @@
 ):
     anywhere = pl.BlockSpec(memory_space=pl.ANY)
     shapes = [((64, 2, 2, 128, 128), BF16), ((64, 128), BF16), ((8, 512), BF16), ((8, 512), BF16)]
+    page_cache, keep_list, fold_weight, table_t, lengths, queries, fresh_entries, out_weight = (
+        pltpu.with_memory_space_constraint(x, pltpu.HBM)
+        for x in (
+            page_cache, keep_list, fold_weight, page_table.T, lengths.reshape(2, 128), queries,
+            fresh_entries, out_weight,
+        )
+    )
+    early = pl.pallas_call(
+        early_kernel,
+        out_shape=pltpu.HBM(*shapes[0]),
+        in_specs=[anywhere] * 5,
+        out_specs=anywhere,
+        scratch_shapes=[
+            pltpu.VMEM((64, 2, 2, 128, 128), BF16),
+            pltpu.VMEM((64, 2, 2, 128, 128), BF16),
+            pltpu.VMEM((64, 128), I32),
+            pltpu.VMEM((64, 128), F32),
+            pltpu.VMEM((8, 256), I32),
+            pltpu.VMEM((2, 128), I32),
+            pltpu.VMEM((64, 128), F32),
+            pltpu.VMEM((64, 128), F32),
+            pltpu.VMEM((3, 64, 128), F32),
+            pltpu.VMEM((64, 128), F32),
+            pltpu.SemaphoreType.DMA((8,)),
+            pltpu.SemaphoreType.DMA((4,)),
+            pltpu.SemaphoreType.DMA((8,)),
+        ],
+        compiler_params=pltpu.CompilerParams(has_side_effects=True, vmem_limit_bytes=36 << 20),
+        name="early",
+    )(page_cache, keep_list, fold_weight, table_t, lengths)
     results = pl.pallas_call(
         main_kernel,
         out_shape=[pltpu.VMEM(shape, dtype) for shape, dtype in shapes],
-        in_specs=[anywhere] * 8,
+        in_specs=[anywhere] * 9,
         out_specs=[pl.BlockSpec(memory_space=pltpu.VMEM)] * 4,
         scratch_shapes=[
             pltpu.VMEM((64, 2, 2, 128, 128), BF16),
@@ -471,24 +576,20 @@
         ),
         name="decode",
     )(
-        *(
-            pltpu.with_memory_space_constraint(x, pltpu.HBM)
-            for x in (
-                page_cache, keep_list, fold_weight, page_table.T, lengths.reshape(2, 128), queries,
-                fresh_entries, out_weight,
-            )
-        )
+        page_cache, keep_list, fold_weight, table_t, lengths, queries, fresh_entries, out_weight,
+        pltpu.with_memory_space_constraint(early, pltpu.HBM),
     )
     return tuple(
         pl.pallas_call(
             write_kernel,
-            out_shape=[jax.ShapeDtypeStruct(shape, dtype) for shape, dtype in shapes],
-            in_specs=[anywhere] * 4,
+            out_shape=[pltpu.HBM(shape, dtype) for shape, dtype in shapes],
+            in_specs=[anywhere] * 5,
             out_specs=[anywhere] * 4,
-            scratch_shapes=[pltpu.SemaphoreType.DMA((12,))],
+            scratch_shapes=[pltpu.SemaphoreType.DMA((11,))],
+            input_output_aliases={4: 0},
             compiler_params=pltpu.CompilerParams(vmem_limit_bytes=1 << 20),
             name="write",
-        )(*results)
+        )(*results, early)
     )
 
 

time: 28.8 us -> 27.5 us (0.955); the launches traced: 28.6 us -> 26.9 us
  Pallas kernels: 27.9 us -> 26.3 us
    pallas_call x1, Pallas kernels: 24.5 us -> 19.4 us  [per_device(): pl.pallas_call(main_kernel, out_shape=[pltpu.VMEM(shape, dtype) for shape...]
    pallas_call x1 -> x2, Pallas kernels: 3.41 us -> 6.91 us  [the longest x1 5.45 us: per_device(): pl.pallas_call(early_kernel, out_shape=pltpu.HBM(*shapes[0]), in_specs=[a...]
where the time goes in v4:
time: 27.5 us; the launch traced here: 26.9 us
  Pallas kernels  26.3 us (96%)
  between operations  0.65 us (2%)
    pallas_call x1, Pallas kernels, per_device(): pl.pallas_call(main_kernel, out_shape=[pltpu.VMEM(shape, dtype) for shape...  19.4 us
    pallas_call x1, Pallas kernels, per_device(): pl.pallas_call(early_kernel, out_shape=pltpu.HBM(*shapes[0]), in_specs=[a...  5.45 us
    pallas_call x1, Pallas kernels, per_device(): pl.pallas_call(write_kernel, out_shape=[pltpu.HBM(shape, dtype) for shape...  1.46 us

profile of v4, /device:TPU:1, one launch (start us, length us, event | category | flops | bytes accessed | tf_op | source)
XLA Modules:
  0.0 26.9 jit_solution(8968447188207981390)
XLA Ops:
  0.6 5.5 %early.1 = bf16[64,2,2,128,128]{4,3,2,1,0:T(8,128)(2,1)} custom-call(bf16[64,2,2,128,128]{4,3,2,1,0:T(8,128)(2,1)} %page_hbm.3, s32[64,128]{1,0:T(8,128)} %keep_hbm.3, f32[64,128]{1,0:T(8,128)} %weight_hbm.3, s32[8,256]{1,0:T(8,128)} %bitcast.2, s32[2,128]{1,0:T(2,128)} %bitcast.4), custom_call_target="tpu_custom_call" | custom-call | tf_op jit(solution)/shard_map/early/pallas_call | solution.py:513
  6.1 19.4 %decode.1 = (bf16[64,2,2,128,128]{4,3,2,1,0:T(8,128)(2,1)S(1)}, bf16[64,128]{1,0:T(8,128)(2,1)S(1)}, bf16[8,512]{1,0:T(8,128)(2,1)S(1)}, bf16[8,512]{1,0:T(8,128)(2,1)S(1)}) custom-call(bf16[64,2,2,128,128]{4,3,2,1,0:T(8,128)(2,1)} %page_hbm.3, s32[64,128]{1,0:T(8,128)} %keep_hbm.3, f32[64,128]{1,0:T(8,128)} %weight_hbm.3, s32[8,256]{1,0:T(8,128)} %bitcast.3, ...), custom_call_target="tpu_custom_call" | custom-call | tf_op jit(solution)/shard_map/decode/pallas_call | solution.py:536
  25.5 1.5 %write.1 = (bf16[64,2,2,128,128]{4,3,2,1,0:T(8,128)(2,1)}, bf16[64,128]{1,0:T(8,128)(2,1)}, bf16[8,512]{1,0:T(8,128)(2,1)}, bf16[8,512]{1,0:T(8,128)(2,1)}) custom-call(bf16[64,2,2,128,128]{4,3,2,1,0:T(8,128)(2,1)S(1)} %get-tuple-element.8.packed, bf16[64,128]{1,0:T(8,128)(2,1)S(1)} %get-tuple-element.9.mass, ...), custom_call_target="tpu_custom_call", output_to_operand_aliasing={{0}: (4, {})} | custom-call | tf_op jit(solution)/shard_map/write/pallas_call | solution.py:583

commit v5 on v4

--- a/solution.py
+++ b/solution.py
@@ -13,8 +13,8 @@
 I32 = jnp.int32
 floor_value = -1e30
 CHUNK = 16
-LEAD = 32
-GROUP = 16
+LEAD = 28
+GROUP = 8
 PEERS = sorted(
     ((dz, dx, dc) for dz in range(4) for dx in range(4) for dc in range(2)),
     key=lambda d: (-min(d[0], 4 - d[0]) - min(d[1], 4 - d[1]), -d[2], d),
@@ -133,7 +133,7 @@
     early,
     packed_ref, mass_ref, attended_ref, projected_ref,
     pages, keep, weight, table, lengths, query, fresh, out_weight,
-    query_flat, fresh_flat, query_send, query_recv, part_send, part_recv, sum_send, sum_recv,
+    query_flat, fresh_flat, query_tiles, query_send, query_recv, part_send, part_recv, sum_send, sum_recv,
     target_rows, count_rows, fold_rows, divisor_rows, mass_rows, score_rows, order_vmem, order,
     page_sem, in_sem, query_send_sem, query_recv_sems, part_sems, sum_sems, order_sem,
 ):
@@ -216,9 +216,10 @@
     )
     for k in range(2):
         for h in range(4):
-            query_send.reshape(256, 128)[pl.ds(k * 4 + h, 32, stride=8), :] = picked[
+            query_tiles.reshape(256, 128)[pl.ds(k * 4 + h, 32, stride=8), :] = picked[
                 k * 32 : k * 32 + 32, h * 128 : h * 128 + 128
             ]
+    query_send[...] = query_tiles[...].astype(BF16)
     def query_copy(k):
         other = at(k)
         return pltpu.make_async_remote_copy(
@@ -230,10 +231,6 @@
             device_id_type=MESH,
         )
 
-    pl.semaphore_wait(barrier, seq_count - 1 + kv_count - 1)
-    for k in range(1, seq_count):
-        query_copy(k).start()
-    query_recv[me] = query_send[me]
 
     request_col = jnp.sum(entry_pick * (lane & 7).astype(F32), axis=1, keepdims=True)
     request_is = ((iota((8, 128), 1) & 7) == iota((8, 128), 0)).astype(F32).astype(BF16)
@@ -256,6 +253,11 @@
     mass = plan_pages(valid_count, keep, weight, rows)
     mass_ref[...] = mass
     mass_rows[...] = mass.astype(F32)
+
+    pl.semaphore_wait(barrier, seq_count - 1 + kv_count - 1)
+    for k in range(1, seq_count):
+        query_copy(k).start()
+    query_recv[me] = query_send[me]
 
     @pl.loop(0, 64 // CHUNK)
     def _(i):
@@ -288,7 +290,7 @@
     def scores(k):
         o = at(k)
         a, b = pages_of(o)
-        q = query_recv[o]
+        q = query_recv[o].astype(F32)
         q = jnp.concatenate(
             [jnp.where(head_low, q, 0.0), jnp.where(head_low, 0.0, q)], axis=1
         ).astype(BF16)
@@ -550,7 +552,8 @@
             pltpu.VMEM((32, 128), F32),
             pltpu.VMEM((32, 128), F32),
             pltpu.VMEM((32, 8, 128), F32),
-            pltpu.VMEM((32, 8, 128), F32),
+            pltpu.VMEM((32, 8, 128), BF16),
+            pltpu.VMEM((32, 8, 128), BF16),
             pltpu.VMEM((32, 16, 128), F32),
             pltpu.VMEM((32, 16, 128), F32),
             pltpu.VMEM((4, 8, 512), BF16),

time: 27.5 us -> 26.4 us (0.960)
  Pallas kernels: 26.3 us -> 25.4 us
    pallas_call x1, Pallas kernels: 19.4 us -> 18.6 us  [per_device(): pl.pallas_call(main_kernel, out_shape=[pltpu.VMEM(shape, dtype) for shape...]
    pallas_call x1, Pallas kernels: 5.45 us -> 4.96 us  [per_device(): pl.pallas_call(early_kernel, out_shape=pltpu.HBM(*shapes[0]), in_specs=[a...]
    pallas_call x1, Pallas kernels: 1.46 us -> 1.8 us  [per_device(): pl.pallas_call(write_kernel, out_shape=[pltpu.HBM(shape, dtype) for shape...]
where the time goes in v5:
time: 26.4 us; the launch traced here: 26.1 us
  Pallas kernels  25.4 us (96%)
  between operations  0.65 us (2%)
    pallas_call x1, Pallas kernels, per_device(): pl.pallas_call(main_kernel, out_shape=[pltpu.VMEM(shape, dtype) for shape...  18.6 us
    pallas_call x1, Pallas kernels, per_device(): pl.pallas_call(early_kernel, out_shape=pltpu.HBM(*shapes[0]), in_specs=[a...  4.96 us
    pallas_call x1, Pallas kernels, per_device(): pl.pallas_call(write_kernel, out_shape=[pltpu.HBM(shape, dtype) for shape...  1.8 us

profile of v5, /device:TPU:1, one launch (start us, length us, event | category | flops | bytes accessed | tf_op | source)
XLA Modules:
  0.0 26.1 jit_solution(13571672022716842142)
XLA Ops:
  0.6 5.0 %early.1 = bf16[64,2,2,128,128]{4,3,2,1,0:T(8,128)(2,1)} custom-call(bf16[64,2,2,128,128]{4,3,2,1,0:T(8,128)(2,1)} %page_hbm.3, s32[64,128]{1,0:T(8,128)} %keep_hbm.3, f32[64,128]{1,0:T(8,128)} %weight_hbm.3, s32[8,256]{1,0:T(8,128)} %bitcast.2, s32[2,128]{1,0:T(2,128)} %bitcast.4), custom_call_target="tpu_custom_call" | custom-call | tf_op jit(solution)/shard_map/early/pallas_call | solution.py:515
  5.6 18.6 %decode.1 = (bf16[64,2,2,128,128]{4,3,2,1,0:T(8,128)(2,1)S(1)}, bf16[64,128]{1,0:T(8,128)(2,1)S(1)}, bf16[8,512]{1,0:T(8,128)(2,1)S(1)}, bf16[8,512]{1,0:T(8,128)(2,1)S(1)}) custom-call(bf16[64,2,2,128,128]{4,3,2,1,0:T(8,128)(2,1)} %page_hbm.3, s32[64,128]{1,0:T(8,128)} %keep_hbm.3, f32[64,128]{1,0:T(8,128)} %weight_hbm.3, s32[8,256]{1,0:T(8,128)} %bitcast.3, ...), custom_call_target="tpu_custom_call" | custom-call | tf_op jit(solution)/shard_map/decode/pallas_call | solution.py:538
  24.2 1.8 %write.1 = (bf16[64,2,2,128,128]{4,3,2,1,0:T(8,128)(2,1)}, bf16[64,128]{1,0:T(8,128)(2,1)}, bf16[8,512]{1,0:T(8,128)(2,1)}, bf16[8,512]{1,0:T(8,128)(2,1)}) custom-call(bf16[64,2,2,128,128]{4,3,2,1,0:T(8,128)(2,1)S(1)} %get-tuple-element.8.packed, bf16[64,128]{1,0:T(8,128)(2,1)S(1)} %get-tuple-element.9.mass, ...), custom_call_target="tpu_custom_call", output_to_operand_aliasing={{0}: (4, {})} | custom-call | tf_op jit(solution)/shard_map/write/pallas_call | solution.py:586

commit v6 on v5

--- a/solution.py
+++ b/solution.py
@@ -14,7 +14,7 @@
 floor_value = -1e30
 CHUNK = 16
 LEAD = 28
-GROUP = 8
+GROUP = 4
 PEERS = sorted(
     ((dz, dx, dc) for dz in range(4) for dx in range(4) for dc in range(2)),
     key=lambda d: (-min(d[0], 4 - d[0]) - min(d[1], 4 - d[1]), -d[2], d),
@@ -392,7 +392,7 @@
     ]
     gather_b = gather.astype(BF16)
     sums = sum(
-        dot(gather_b, piece) for piece in split(jnp.concatenate(scaled + [factor * total], axis=1), 3)
+        dot(gather_b, piece) for piece in split(jnp.concatenate(scaled + [factor * total], axis=1), 2)
     )
     own_factor = jnp.exp(own - best)
     denominator = sums[:, 512:] + own_factor

time: 26.4 us -> 26.4 us (level)
  no operation moved by 1% of the time
where the time goes in v6:
time: 26.4 us; the launch traced here: 26 us
  Pallas kernels  25.3 us (96%)
  between operations  0.65 us (2%)
    pallas_call x1, Pallas kernels, per_device(): pl.pallas_call(main_kernel, out_shape=[pltpu.VMEM(shape, dtype) for shape...  18.6 us
    pallas_call x1, Pallas kernels, per_device(): pl.pallas_call(early_kernel, out_shape=pltpu.HBM(*shapes[0]), in_specs=[a...  4.96 us
    pallas_call x1, Pallas kernels, per_device(): pl.pallas_call(write_kernel, out_shape=[pltpu.HBM(shape, dtype) for shape...  1.8 us

profile of v6, /device:TPU:1, one launch (start us, length us, event | category | flops | bytes accessed | tf_op | source)
XLA Modules:
  0.0 26.0 jit_solution(9928702935832151964)
XLA Ops:
  0.6 5.0 %early.1 = bf16[64,2,2,128,128]{4,3,2,1,0:T(8,128)(2,1)} custom-call(bf16[64,2,2,128,128]{4,3,2,1,0:T(8,128)(2,1)} %page_hbm.3, s32[64,128]{1,0:T(8,128)} %keep_hbm.3, f32[64,128]{1,0:T(8,128)} %weight_hbm.3, s32[8,256]{1,0:T(8,128)} %bitcast.2, s32[2,128]{1,0:T(2,128)} %bitcast.4), custom_call_target="tpu_custom_call" | custom-call | tf_op jit(solution)/shard_map/early/pallas_call | solution.py:515
  5.6 18.6 %decode.1 = (bf16[64,2,2,128,128]{4,3,2,1,0:T(8,128)(2,1)S(1)}, bf16[64,128]{1,0:T(8,128)(2,1)S(1)}, bf16[8,512]{1,0:T(8,128)(2,1)S(1)}, bf16[8,512]{1,0:T(8,128)(2,1)S(1)}) custom-call(bf16[64,2,2,128,128]{4,3,2,1,0:T(8,128)(2,1)} %page_hbm.3, s32[64,128]{1,0:T(8,128)} %keep_hbm.3, f32[64,128]{1,0:T(8,128)} %weight_hbm.3, s32[8,256]{1,0:T(8,128)} %bitcast.3, ...), custom_call_target="tpu_custom_call" | custom-call | tf_op jit(solution)/shard_map/decode/pallas_call | solution.py:538
  24.2 1.8 %write.1 = (bf16[64,2,2,128,128]{4,3,2,1,0:T(8,128)(2,1)}, bf16[64,128]{1,0:T(8,128)(2,1)}, bf16[8,512]{1,0:T(8,128)(2,1)}, bf16[8,512]{1,0:T(8,128)(2,1)}) custom-call(bf16[64,2,2,128,128]{4,3,2,1,0:T(8,128)(2,1)S(1)} %get-tuple-element.8.packed, bf16[64,128]{1,0:T(8,128)(2,1)S(1)} %get-tuple-element.9.mass, ...), custom_call_target="tpu_custom_call", output_to_operand_aliasing={{0}: (4, {})} | custom-call | tf_op jit(solution)/shard_map/write/pallas_call | solution.py:586

commit v7 on v5

--- a/solution.py
+++ b/solution.py
@@ -13,7 +13,7 @@
 I32 = jnp.int32
 floor_value = -1e30
 CHUNK = 16
-LEAD = 28
+LEAD = 25
 GROUP = 8
 PEERS = sorted(
     ((dz, dx, dc) for dz in range(4) for dx in range(4) for dc in range(2)),

time: 26.4 us -> 26.7 us (1.011)
  the two profiles are of different devices: /device:TPU:1 before, /device:TPU:24 now
where the time goes in v7:
time: 26.7 us; the launch traced here: 26.5 us
  Pallas kernels  25.8 us (97%)
  between operations  0.65 us (2%)
    pallas_call x1, Pallas kernels, per_device(): pl.pallas_call(main_kernel, out_shape=[pltpu.VMEM(shape, dtype) for shape...  19.7 us
    pallas_call x1, Pallas kernels, per_device(): pl.pallas_call(write_kernel, out_shape=[pltpu.HBM(shape, dtype) for shape...  3.12 us
    pallas_call x1, Pallas kernels, per_device(): pl.pallas_call(early_kernel, out_shape=pltpu.HBM(*shapes[0]), in_specs=[a...  2.97 us

profile of v7, /device:TPU:24, one launch (start us, length us, event | category | flops | bytes accessed | tf_op | source)
XLA Modules:
  0.0 26.5 jit_solution(17195625138858328720)
XLA Ops:
  0.6 3.0 %early.1 = bf16[64,2,2,128,128]{4,3,2,1,0:T(8,128)(2,1)} custom-call(bf16[64,2,2,128,128]{4,3,2,1,0:T(8,128)(2,1)} %page_hbm.3, s32[64,128]{1,0:T(8,128)} %keep_hbm.3, f32[64,128]{1,0:T(8,128)} %weight_hbm.3, s32[8,256]{1,0:T(8,128)} %bitcast.2, s32[2,128]{1,0:T(2,128)} %bitcast.4), custom_call_target="tpu_custom_call" | custom-call | tf_op jit(solution)/shard_map/early/pallas_call | solution.py:515
  3.6 19.7 %decode.1 = (bf16[64,2,2,128,128]{4,3,2,1,0:T(8,128)(2,1)S(1)}, bf16[64,128]{1,0:T(8,128)(2,1)S(1)}, bf16[8,512]{1,0:T(8,128)(2,1)S(1)}, bf16[8,512]{1,0:T(8,128)(2,1)S(1)}) custom-call(bf16[64,2,2,128,128]{4,3,2,1,0:T(8,128)(2,1)} %page_hbm.3, s32[64,128]{1,0:T(8,128)} %keep_hbm.3, f32[64,128]{1,0:T(8,128)} %weight_hbm.3, s32[8,256]{1,0:T(8,128)} %bitcast.3, ...), custom_call_target="tpu_custom_call" | custom-call | tf_op jit(solution)/shard_map/decode/pallas_call | solution.py:538
  23.4 3.1 %write.1 = (bf16[64,2,2,128,128]{4,3,2,1,0:T(8,128)(2,1)}, bf16[64,128]{1,0:T(8,128)(2,1)}, bf16[8,512]{1,0:T(8,128)(2,1)}, bf16[8,512]{1,0:T(8,128)(2,1)}) custom-call(bf16[64,2,2,128,128]{4,3,2,1,0:T(8,128)(2,1)S(1)} %get-tuple-element.8.packed, bf16[64,128]{1,0:T(8,128)(2,1)S(1)} %get-tuple-element.9.mass, ...), custom_call_target="tpu_custom_call", output_to_operand_aliasing={{0}: (4, {})} | custom-call | tf_op jit(solution)/shard_map/write/pallas_call | solution.py:586
